TPU v7x, 512 devices: a whole 4x8x8 slice. The times are simulated.
512 devices in a mesh: tm: 8 (over x, core), row: 64 (over z, y).
Axes of the slice: x: 4, y: 8, z: 8, core: 2. Of those that a mesh axis runs over, the one named last changes fastest.
Arguments:
- snapshots: float32 [65536, 1024], P('row', 'tm'), may hold values from -6 to 6
- sketches: float32 [3, 256, 128], replicated, may hold values from -0.375 to 0.375
Outputs:
- coefficients: float32 [128, 1024], P(None, 'tm')
- deflated: float32 [65536, 1024], P('row', 'tm')
All inputs are finite; a program needn't handle non-finite values.
Results may differ from a plain program's by a relative error of at most 0.00024.
Values sent between devices are 32-bit elements; how exact they have to be, the bound alone decides.
A program may use at most 64 MiB of HBM per device.

v0:
```python
import jax
import jax.numpy as jnp
from jax import lax
from jax.sharding import PartitionSpec as P

NS_STEPS = 5


HIGH = lax.Precision.HIGHEST


def rows_for(lines, count):
    spare = -lines.shape[0] % count
    if not spare:
        return lines
    return jnp.concatenate([lines, jnp.zeros((spare, *lines.shape[1:]), lines.dtype)])


def joined_along(tiles, dim):
    tiles = jnp.moveaxis(tiles, 0, dim)
    shape = tiles.shape
    return tiles.reshape(*shape[:dim], shape[dim] * shape[dim + 1], *shape[dim + 2 :])


def from_everyone(x, axis):
    count = lax.axis_size(axis)
    return lax.all_to_all(jnp.broadcast_to(x[None], (count, *x.shape)), axis, 0, 0, tiled=True)


def gather_directly(x, axis, dim):
    return joined_along(from_everyone(x, axis), dim)


def split_up(x, dim, count):
    before, after = (x.shape[:dim], x.shape[dim + 1 :])
    return jnp.moveaxis(x.reshape(*before, count, -1, *after), dim, 0)


def sum_at_owner(x, axis, dim):
    tiles = split_up(x, dim, lax.axis_size(axis))
    arrived = lax.all_to_all(tiles, axis, split_axis=0, concat_axis=0, tiled=True)
    return arrived.sum(axis=0)


def sum_by_parts(x, axes):
    lines = x.reshape(-1, x.shape[-1])
    padded = rows_for(lines, lax.axis_size(axes))
    whole = gather_directly(sum_at_owner(padded, axes, 0), axes, 0)
    return lax.slice_in_dim(whole, 0, len(lines)).reshape(x.shape)


def passed_along(block, axis, distance):
    devices = range(lax.axis_size(axis))
    route = [((i - distance) % len(devices), i) for i in devices]
    return lax.ppermute(block, axis, route)


def product_t(left, right):
    return jnp.dot(left.T, right, precision=HIGH, preferred_element_type=jnp.float32)


def product(left, right):
    return jnp.dot(left, right, precision=HIGH, preferred_element_type=jnp.float32)


def inverse_root(matrix):
    frob_scale = jnp.sqrt(jnp.sum(matrix * matrix) + 1e-06)
    ident = jnp.eye(matrix.shape[0], dtype=matrix.dtype)
    y_iter = matrix / frob_scale
    z_iter = ident
    for repeat in range(NS_STEPS):
        middle = 1.5 * ident - 0.5 * product(z_iter, y_iter)
        y_iter = product(y_iter, middle)
        z_iter = product(middle, z_iter)
    return z_iter / jnp.sqrt(frob_scale)


def body(snapshots, sketches):
    leaf_sum = sum_by_parts(product_t(snapshots, snapshots), "row")
    leaf_root = inverse_root(leaf_sum)
    mode_block = product(snapshots, leaf_root)
    own_gram = product_t(leaf_root, product(leaf_sum, leaf_root))
    group_count = lax.axis_size("tm")
    tree_depth = group_count.bit_length() - 1
    for tree_level in range(tree_depth):
        sketch = sketches[tree_level]
        lower_block, lower_gram = passed_along((mode_block, own_gram), "tm", 1 << tree_level)
        cross_sum = sum_by_parts(product_t(lower_block, mode_block), "row")
        top_rows = jnp.concatenate([lower_gram, cross_sum], axis=1)
        bottom_rows = jnp.concatenate([cross_sum.T, own_gram], axis=1)
        gram_sum = jnp.concatenate([top_rows, bottom_rows], axis=0)
        joined = jnp.concatenate([lower_block, mode_block], axis=1)
        reduced = product(gram_sum, sketch)
        small = product_t(reduced, product(gram_sum, reduced))
        mixing = product(reduced, inverse_root(small))
        mode_block = product(joined, mixing)
        own_gram = product_t(mixing, product(gram_sum, mixing))
    coefficients = sum_by_parts(product_t(mode_block, snapshots), "row")
    deflated = snapshots - product(mode_block, coefficients)
    return (coefficients, deflated)


def solution(mesh):
    placed = (P("row", "tm"), P())
    return jax.shard_map(
        body, mesh=mesh, in_specs=placed, out_specs=(P(None, "tm"), P("row", "tm")), check_vma=False
    )
```

profile of v0, /device:TPU:8, one launch (start us, length us, event | category | flops | bytes accessed | tf_op | source)
XLA Modules:
  0.0 260.9 jit_solution(9402026192420046888)
XLA Ops:
  0.6 2.2 fusion.66
  2.8 27.8 %all_to_all.50 = f32[64,2,128]{2,1,0:T(2,128)S(1)} all-to-all(f32[64,2,128]{2,1,0:T(2,128)S(1)} %bitcast.182), channel_id=1, replica_groups=mesh['tm'=8,'row'=64] {'row'}, dimensions={0} | all-to-all | bytes 131072 | tf_op jit(solution)/shard_map/all_to_all | solution.py:41
  30.7 16.0 %all_to_all.51 = f32[64,2,128]{2,1,0:T(2,128)S(1)} all-to-all(f32[64,2,128]{2,1,0:T(2,128)S(1)} %broadcast_in_dim.10), channel_id=1, replica_groups=mesh['tm'=8,'row'=64] {'row'}, dimensions={0} | all-to-all | bytes 131072 | tf_op jit(solution)/shard_map/all_to_all | solution.py:27
  51.7 9.8 %collective-permute-done = f32[1024,128]{0,1:T(8,128)S(1)} collective-permute-done((f32[1024,128]{0,1:T(8,128)S(1)}, f32[1024,128]{0,1:T(8,128)S(1)}, u32[]{:S(2)}, u32[]{:S(2)}) %collective-permute-start) | collective-permute-done | bytes 524320 | tf_op jit(solution)/shard_map/ppermute | solution.py:55
  61.5 1.2 fusion.76
  62.7 5.4 %all-to-all-start.2 = ((f32[64,2,128]{2,1,0:T(2,128)}), f32[64,2,128]{2,1,0:T(2,128)S(1)}, u32[]{:S(2)}, u32[]{:S(2)}) async-start(f32[64,2,128]{2,1,0:T(2,128)} %bitcast.3), calls=%async_computation.2 | async-start | bytes 131072 | tf_op jit(solution)/shard_map/all_to_all | solution.py:41
  68.3 11.3 %all-to-all-done.2 = f32[64,2,128]{2,1,0:T(2,128)S(1)} async-done(((f32[64,2,128]{2,1,0:T(2,128)}), f32[64,2,128]{2,1,0:T(2,128)S(1)}, u32[]{:S(2)}, u32[]{:S(2)}) %all-to-all-start.2) | async-done | bytes 65568 | tf_op jit(solution)/shard_map/all_to_all | solution.py:41
  80.3 5.4 %all-to-all-start.3 = ((f32[64,2,128]{2,1,0:T(2,128)}), f32[64,2,128]{2,1,0:T(2,128)S(1)}, u32[]{:S(2)}, u32[]{:S(2)}) async-start(f32[64,2,128]{2,1,0:T(2,128)} %broadcast_in_dim.11), calls=%async_computation.3 | async-start | bytes 131072 | tf_op jit(solution)/shard_map/all_to_all | solution.py:27
  86.0 11.2 %all-to-all-done.3 = f32[64,2,128]{2,1,0:T(2,128)S(1)} async-done(((f32[64,2,128]{2,1,0:T(2,128)}), f32[64,2,128]{2,1,0:T(2,128)S(1)}, u32[]{:S(2)}, u32[]{:S(2)}) %all-to-all-start.3) | async-done | bytes 65568 | tf_op jit(solution)/shard_map/all_to_all | solution.py:27
  98.5 1.0 multiply_reduce_fusion.2
  104.2 2.2 collective-permute-start.2
  106.4 10.3 %collective-permute-done.2 = f32[1024,128]{0,1:T(8,128)S(1)} collective-permute-done((f32[1024,128]{0,1:T(8,128)S(1)}, f32[1024,128]{0,1:T(8,128)S(1)}, u32[]{:S(2)}, u32[]{:S(2)}) %collective-permute-start.2) | collective-permute-done | bytes 524320 | tf_op jit(solution)/shard_map/ppermute | solution.py:55
  116.7 1.2 fusion.85
  117.9 7.7 %all-to-all-start.4 = ((f32[64,2,128]{2,1,0:T(2,128)}), f32[64,2,128]{2,1,0:T(2,128)S(1)}, u32[]{:S(2)}, u32[]{:S(2)}) async-start(f32[64,2,128]{2,1,0:T(2,128)} %bitcast.7), calls=%async_computation.4 | async-start | bytes 131072 | tf_op jit(solution)/shard_map/all_to_all | solution.py:41
  126.2 10.8 %all-to-all-done.4 = f32[64,2,128]{2,1,0:T(2,128)S(1)} async-done(((f32[64,2,128]{2,1,0:T(2,128)}), f32[64,2,128]{2,1,0:T(2,128)S(1)}, u32[]{:S(2)}, u32[]{:S(2)}) %all-to-all-start.4) | async-done | bytes 65568 | tf_op jit(solution)/shard_map/all_to_all | solution.py:41
  137.7 5.3 %all-to-all-start.5 = ((f32[64,2,128]{2,1,0:T(2,128)}), f32[64,2,128]{2,1,0:T(2,128)S(1)}, u32[]{:S(2)}, u32[]{:S(2)}) async-start(f32[64,2,128]{2,1,0:T(2,128)} %broadcast_in_dim.12), calls=%async_computation.5 | async-start | bytes 131072 | tf_op jit(solution)/shard_map/all_to_all | solution.py:27
  143.5 2.2 collective-permute-start.3
  145.6 8.9 %all-to-all-done.5 = f32[64,2,128]{2,1,0:T(2,128)S(1)} async-done(((f32[64,2,128]{2,1,0:T(2,128)}), f32[64,2,128]{2,1,0:T(2,128)S(1)}, u32[]{:S(2)}, u32[]{:S(2)}) %all-to-all-start.5) | async-done | bytes 65568 | tf_op jit(solution)/shard_map/all_to_all | solution.py:27
  155.9 1.0 multiply_reduce_fusion.1
  161.5 3.6 %collective-permute-start.4 = (f32[1024,128]{0,1:T(8,128)S(1)}, f32[1024,128]{0,1:T(8,128)S(1)}, u32[]{:S(2)}, u32[]{:S(2)}) collective-permute-start(f32[1024,128]{0,1:T(8,128)S(1)} %fusion.24), channel_id=1, source_target_pairs={{256,0},{320,64},{384,128},{448,192},{0,256},{64,320},{128,384},{1... | collective-permute-start | bytes 1572872 | tf_op jit(solution)/shard_map/ppermute | solution.py:55
  165.2 8.9 %collective-permute-done.4 = f32[1024,128]{0,1:T(8,128)S(1)} collective-permute-done((f32[1024,128]{0,1:T(8,128)S(1)}, f32[1024,128]{0,1:T(8,128)S(1)}, u32[]{:S(2)}, u32[]{:S(2)}) %collective-permute-start.4) | collective-permute-done | bytes 524320 | tf_op jit(solution)/shard_map/ppermute | solution.py:55
  174.1 1.2 fusion.94
  175.3 9.0 %all-to-all-start.6 = ((f32[64,2,128]{2,1,0:T(2,128)}), f32[64,2,128]{2,1,0:T(2,128)S(1)}, u32[]{:S(2)}, u32[]{:S(2)}) async-start(f32[64,2,128]{2,1,0:T(2,128)} %bitcast.11), calls=%async_computation.6 | async-start | bytes 131072 | tf_op jit(solution)/shard_map/all_to_all | solution.py:41
  184.9 10.8 %all-to-all-done.6 = f32[64,2,128]{2,1,0:T(2,128)S(1)} async-done(((f32[64,2,128]{2,1,0:T(2,128)}), f32[64,2,128]{2,1,0:T(2,128)S(1)}, u32[]{:S(2)}, u32[]{:S(2)}) %all-to-all-start.6) | async-done | bytes 65568 | tf_op jit(solution)/shard_map/all_to_all | solution.py:41
  196.4 5.3 %all-to-all-start.7 = ((f32[64,2,128]{2,1,0:T(2,128)}), f32[64,2,128]{2,1,0:T(2,128)S(1)}, u32[]{:S(2)}, u32[]{:S(2)}) async-start(f32[64,2,128]{2,1,0:T(2,128)} %broadcast_in_dim.13), calls=%async_computation.7 | async-start | bytes 131072 | tf_op jit(solution)/shard_map/all_to_all | solution.py:27
  202.2 2.4 collective-permute-start.5
  204.5 8.7 %all-to-all-done.7 = f32[64,2,128]{2,1,0:T(2,128)S(1)} async-done(((f32[64,2,128]{2,1,0:T(2,128)}), f32[64,2,128]{2,1,0:T(2,128)S(1)}, u32[]{:S(2)}, u32[]{:S(2)}) %all-to-all-start.7) | async-done | bytes 65568 | tf_op jit(solution)/shard_map/all_to_all | solution.py:27
  219.5 1.8 fusion.28
  221.3 1.0 fusion.102
  222.3 20.4 %all_to_all.52 = f32[64,2,128]{2,1,0:T(2,128)S(1)} all-to-all(f32[64,2,128]{2,1,0:T(2,128)S(1)} %bitcast.183), channel_id=1, replica_groups=mesh['tm'=8,'row'=64] {'row'}, dimensions={0} | all-to-all | bytes 131072 | tf_op jit(solution)/shard_map/all_to_all | solution.py:41
  242.9 16.0 %all_to_all.53 = f32[64,2,128]{2,1,0:T(2,128)S(1)} all-to-all(f32[64,2,128]{2,1,0:T(2,128)S(1)} %broadcast_in_dim.14), channel_id=1, replica_groups=mesh['tm'=8,'row'=64] {'row'}, dimensions={0} | all-to-all | bytes 131072 | tf_op jit(solution)/shard_map/all_to_all | solution.py:27
  258.9 1.4 convolution_subtract_fusion
  (99 shorter events, 25.1 us)
Async XLA Ops:
  49.9 1.1 copy-start
  51.7 9.8 %collective-permute-start = (f32[1024,128]{0,1:T(8,128)S(1)}, f32[1024,128]{0,1:T(8,128)S(1)}, u32[]{:S(2)}, u32[]{:S(2)}) collective-permute-start(f32[1024,128]{0,1:T(8,128)S(1)} %bitcast.164), channel_id=1, source_target_pairs={{448,0},{0,64},{64,128},{128,192},{192,256},{256,320},{320,384},{3... | collective-permute-start | bytes 1572872 | tf_op jit(solution)/shard_map/ppermute | solution.py:55
  62.7 16.8 %all-to-all-start.2 = ((f32[64,2,128]{2,1,0:T(2,128)}), f32[64,2,128]{2,1,0:T(2,128)S(1)}, u32[]{:S(2)}, u32[]{:S(2)}) async-start(f32[64,2,128]{2,1,0:T(2,128)} %bitcast.3), calls=%async_computation.2 | async-start | bytes 131072 | tf_op jit(solution)/shard_map/all_to_all | solution.py:41
  68.1 29.2 %copy-start.1 = (f32[3,256,128]{2,1,0:T(8,128)S(1)}, f32[3,256,128]{2,1,0:T(8,128)}, u32[]{:S(2)}) copy-start(f32[3,256,128]{2,1,0:T(8,128)} %param.3) | copy-start | bytes 1179652
  80.3 16.9 %all-to-all-start.3 = ((f32[64,2,128]{2,1,0:T(2,128)}), f32[64,2,128]{2,1,0:T(2,128)S(1)}, u32[]{:S(2)}, u32[]{:S(2)}) async-start(f32[64,2,128]{2,1,0:T(2,128)} %broadcast_in_dim.11), calls=%async_computation.3 | async-start | bytes 131072 | tf_op jit(solution)/shard_map/all_to_all | solution.py:27
  86.0 11.3 %collective-permute-start.1 = (f32[128,128]{0,1:T(8,128)S(1)}, f32[128,128]{0,1:T(8,128)S(1)}, u32[]{:S(2)}, u32[]{:S(2)}) collective-permute-start(f32[128,128]{0,1:T(8,128)S(1)} %fusion.75), channel_id=1, source_target_pairs={{448,0},{0,64},{64,128},{128,192},{192,256},{256,320},{320,384},{3... | collective-permute-start | bytes 196616 | tf_op jit(solution)/shard_map/ppermute | solution.py:55
  104.2 12.5 %collective-permute-start.2 = (f32[1024,128]{0,1:T(8,128)S(1)}, f32[1024,128]{0,1:T(8,128)S(1)}, u32[]{:S(2)}, u32[]{:S(2)}) collective-permute-start(f32[1024,128]{0,1:T(8,128)S(1)} %fusion.20), channel_id=1, source_target_pairs={{384,0},{448,64},{0,128},{64,192},{128,256},{192,320},{256,384},{3... | collective-permute-start | bytes 1572872 | tf_op jit(solution)/shard_map/ppermute | solution.py:55
  117.9 19.1 %all-to-all-start.4 = ((f32[64,2,128]{2,1,0:T(2,128)}), f32[64,2,128]{2,1,0:T(2,128)S(1)}, u32[]{:S(2)}, u32[]{:S(2)}) async-start(f32[64,2,128]{2,1,0:T(2,128)} %bitcast.7), calls=%async_computation.4 | async-start | bytes 131072 | tf_op jit(solution)/shard_map/all_to_all | solution.py:41
  137.7 16.9 %all-to-all-start.5 = ((f32[64,2,128]{2,1,0:T(2,128)}), f32[64,2,128]{2,1,0:T(2,128)S(1)}, u32[]{:S(2)}, u32[]{:S(2)}) async-start(f32[64,2,128]{2,1,0:T(2,128)} %broadcast_in_dim.12), calls=%async_computation.5 | async-start | bytes 131072 | tf_op jit(solution)/shard_map/all_to_all | solution.py:27
  143.5 11.2 %collective-permute-start.3 = (f32[128,128]{0,1:T(8,128)S(1)}, f32[128,128]{0,1:T(8,128)S(1)}, u32[]{:S(2)}, u32[]{:S(2)}) collective-permute-start(f32[128,128]{0,1:T(8,128)S(1)} %fusion.84), channel_id=1, source_target_pairs={{384,0},{448,64},{0,128},{64,192},{128,256},{192,320},{256,384},{3... | collective-permute-start | bytes 196616 | tf_op jit(solution)/shard_map/ppermute | solution.py:55
  161.5 12.6 %collective-permute-start.4 = (f32[1024,128]{0,1:T(8,128)S(1)}, f32[1024,128]{0,1:T(8,128)S(1)}, u32[]{:S(2)}, u32[]{:S(2)}) collective-permute-start(f32[1024,128]{0,1:T(8,128)S(1)} %fusion.24), channel_id=1, source_target_pairs={{256,0},{320,64},{384,128},{448,192},{0,256},{64,320},{128,384},{1... | collective-permute-start | bytes 1572872 | tf_op jit(solution)/shard_map/ppermute | solution.py:55
  175.3 20.4 %all-to-all-start.6 = ((f32[64,2,128]{2,1,0:T(2,128)}), f32[64,2,128]{2,1,0:T(2,128)S(1)}, u32[]{:S(2)}, u32[]{:S(2)}) async-start(f32[64,2,128]{2,1,0:T(2,128)} %bitcast.11), calls=%async_computation.6 | async-start | bytes 131072 | tf_op jit(solution)/shard_map/all_to_all | solution.py:41
  196.4 16.9 %all-to-all-start.7 = ((f32[64,2,128]{2,1,0:T(2,128)}), f32[64,2,128]{2,1,0:T(2,128)S(1)}, u32[]{:S(2)}, u32[]{:S(2)}) async-start(f32[64,2,128]{2,1,0:T(2,128)} %broadcast_in_dim.13), calls=%async_computation.7 | async-start | bytes 131072 | tf_op jit(solution)/shard_map/all_to_all | solution.py:27
  202.2 11.2 %collective-permute-start.5 = (f32[128,128]{0,1:T(8,128)S(1)}, f32[128,128]{0,1:T(8,128)S(1)}, u32[]{:S(2)}, u32[]{:S(2)}) collective-permute-start(f32[128,128]{0,1:T(8,128)S(1)} %fusion.93), channel_id=1, source_target_pairs={{256,0},{320,64},{384,128},{448,192},{0,256},{64,320},{128,384},{1... | collective-permute-start | bytes 196616 | tf_op jit(solution)/shard_map/ppermute | solution.py:55
where the time goes:
time: 262 us; the launch traced here: 261 us
  waiting for transfers between devices  90.8 us (35%)
  blocking collectives  80.3 us (31%)
  starting transfers between devices  48.5 us (19%)
  matrix products  33.1 us (13%)
  between operations  4.35 us (2%)
  local copies, waits for them, and re-layouts  2.9 us (1%)
    all_to_all x2, blocking collectives, sum_at_owner(): lax.all_to_all(tiles, axis, split_axis=0, concat_axis=0, tiled=True)  48.2 us
    all_to_all x3, waiting for transfers between devices, sum_at_owner(): lax.all_to_all(tiles, axis, split_axis=0, concat_axis=0, tiled=True)  32.8 us
    all_to_all x2, blocking collectives, from_everyone(): lax.all_to_all(jnp.broadcast_to(x[None], (count, *x.shape)), axis, 0, 0,...  32 us
    ppermute x6, waiting for transfers between devices, passed_along(): return lax.ppermute(block, axis, route)  29.1 us
    all_to_all x3, waiting for transfers between devices, from_everyone(): lax.all_to_all(jnp.broadcast_to(x[None], (count, *x.shape)), axis, 0, 0,...  28.8 us
    dot_general x73, matrix products, product(): jnp.dot(left, right, precision=HIGH, preferred_element_type=jnp.float32)  22.3 us
    all_to_all x3, starting transfers between devices, sum_at_owner(): lax.all_to_all(tiles, axis, split_axis=0, concat_axis=0, tiled=True)  22 us
    all_to_all x3, starting transfers between devices, from_everyone(): lax.all_to_all(jnp.broadcast_to(x[None], (count, *x.shape)), axis, 0, 0,...  16.1 us
  transfers between devices with their start and end apart: 12, of which 9 were waited for; matrix products, arithmetic and copies ran while one was open for 1% of the time, Pallas kernels for 0%

commit v1 on v0

v1 whole, which is shorter than its diff:
```python
import functools

import jax
import jax.numpy as jnp
from jax import lax
from jax.experimental import pallas as pl
from jax.experimental.pallas import tpu as pltpu
from jax.sharding import PartitionSpec as P

BF, F32 = jnp.bfloat16, jnp.float32
MESH = pl.DeviceIdType.MESH
NX, NC, NY, NZ = 4, 2, 8, 8
N = 128
ROWS = 1024
HALF = ROWS // 2


def split(a):
    high = a.astype(BF)
    return high, (a - high.astype(F32)).astype(BF)


def mm(a, b):
    ah, al = split(a)
    bh, bl = split(b)
    left = jnp.concatenate([ah, ah, al], 1)
    right = jnp.concatenate([bh, bl, bh], 0)
    return jnp.dot(left, right, preferred_element_type=F32)


def identity():
    down = lax.broadcasted_iota(jnp.int32, (N, N), 0)
    across = lax.broadcasted_iota(jnp.int32, (N, N), 1)
    return jnp.where(down == across, 1.0, 0.0).astype(F32)


def inverse_roots(grams, want_image=True):
    one = identity()
    scales = [jnp.sqrt(jnp.sum(a * a, keepdims=True) + 1e-06) for a in grams]
    ts = [a / s for a, s in zip(grams, scales)]
    zs = ms = [1.5 * one - 0.5 * t for t in ts]
    ts = [mm(mm(t, m), m) for t, m in zip(ts, ms)]
    for step in range(1, 5):
        ms = [1.5 * one - 0.5 * t for t in ts]
        if step == 4 and not want_image:
            zs = [mm(z, m) for z, m in zip(zs, ms)]
        else:
            both = [mm(jnp.concatenate([t, z], 0), m) for t, z, m in zip(ts, zs, ms)]
            zs = [b[N:] for b in both]
            ts = [mm(b[:N], m) for b, m in zip(both, ms)]
    return [z / jnp.sqrt(s) for z, s in zip(zs, scales)], ts


def sketched(t_p, t_g, cross, sketch):
    top = jnp.concatenate([t_p, cross.T], 1)
    bottom = jnp.concatenate([cross, t_g], 1)
    gram = jnp.concatenate([top, bottom], 0)
    s = mm(gram, sketch)
    return s, mm(s.T, mm(gram, s))


def tree(root, image, block, own, sketch, x_of):
    r = [root(o) for o in range(8)]
    s0, a0, e0 = [], [], []
    for j in range(4):
        cross = mm(mm(r[2 * j], block(2 * j, 2 * j + 1)), r[2 * j + 1])
        s, a = sketched(image(2 * j + 1), image(2 * j), cross, sketch(0))
        s0.append(s)
        a0.append(a)
    for j in range(4):
        e0.append(jnp.concatenate([mm(r[2 * j + 1], s0[j][:N]), mm(r[2 * j], s0[j][N:])], 0))
    cross1 = []
    for j in range(0, 4, 2):
        upper = jnp.concatenate([block(2 * j + 1, 2 * j + 3), block(2 * j + 1, 2 * j + 2)], 1)
        lower = jnp.concatenate([block(2 * j, 2 * j + 3), block(2 * j, 2 * j + 2)], 1)
        cross1.append(mm(e0[j].T, mm(jnp.concatenate([upper, lower], 0), e0[j + 1])))
    r1, t1 = inverse_roots(a0)
    s1, a1, e1 = [], [], []
    for j in range(2):
        cross = mm(mm(r1[2 * j], cross1[j]), r1[2 * j + 1])
        s, a = sketched(t1[2 * j + 1], t1[2 * j], cross, sketch(1))
        s1.append(s)
        a1.append(a)
    for j in range(2):
        upper = mm(e0[2 * j + 1], mm(r1[2 * j + 1], s1[j][:N]))
        lower = mm(e0[2 * j], mm(r1[2 * j], s1[j][N:]))
        e1.append(jnp.concatenate([upper, lower], 0))
    wide = [jnp.concatenate([block(a, b) for b in (7, 6, 5, 4)], 1) for a in (3, 2, 1, 0)]
    cross2 = mm(e1[0].T, mm(jnp.concatenate(wide, 0), e1[1]))
    near = jnp.concatenate([block(0, 3), block(0, 2), block(0, 1), own], 1)
    far = jnp.concatenate([block(0, 7), block(0, 6), block(0, 5), block(0, 4)], 1)
    w_far, w_near = mm(far, e1[1]), mm(near, e1[0])
    r2, t2 = inverse_roots(a1)
    s2, a2 = sketched(t2[1], t2[0], mm(mm(r2[0], cross2), r2[1]), sketch(2))
    h = mm(jnp.concatenate([mm(w_far, r2[1]), mm(w_near, r2[0])], 1), s2)
    upper = mm(e1[1], mm(r2[1], s2[:N]))
    lower = mm(e1[0], mm(r2[0], s2[N:]))
    x_all = jnp.concatenate([x_of(o) for o in range(7, -1, -1)], 1)
    base = mm(x_all, jnp.concatenate([upper, lower], 0))
    r3 = inverse_roots([a2], False)[0][0]
    coefficients = mm(h, r3).T
    return coefficients, x_of(0) - mm(base, mm(r3, coefficients))


def place():
    tm, row = lax.axis_index("tm"), lax.axis_index("row")
    return tm // NC, tm % NC, row % NY, row // NY


def device(x, c, y, z):
    return (x * NC + c, z * NY + y)


def rows_of(index, count):
    return pl.ds(pl.multiple_of(index * count, count), count)


def exchange(x_ref, xall, kall, rt, own, part, rsy, rsz, zsrc, lrow, lsy, lsz, leaves,
             g_s, g_r, c_s, c_r, y_s, y_r, z_s, z_r, p1_s, p1_r, p2_s, p2_r, p3_s, p3_r, p4_s, p4_r,
             ly_s, ly_r, lz_s, lz_r, la_s, la_r, b1_s, b1_r, b2_s, b2_r, b4_s, b4_r):
    x, c, y, z = place()
    left, right, across = (x + 3) % NX, (x + 1) % NX, (x + 2) % NX
    peers_x = [device((x + k) % NX, c, y, z) for k in range(1, NX)]
    peers_y = [device(x, c, (y + k) % NY, z) for k in range(1, NY)]
    peers_z = [device(x, c, y, (z + k) % NZ) for k in range(1, NZ)]
    partner = device(x, 1 - c, y, z)

    barrier = pltpu.get_barrier_semaphore()
    everyone = peers_x + peers_y + peers_z + [partner]
    for peer in everyone:
        pl.semaphore_signal(barrier, inc=1, device_id=peer, device_id_type=MESH)
    pl.semaphore_wait(barrier, len(everyone))

    def send(src, dst, s, r, peer):
        copy = pltpu.make_async_remote_copy(
            src_ref=src, dst_ref=dst, send_sem=s, recv_sem=r, device_id=peer, device_id_type=MESH
        )
        copy.start()
        return copy

    pending = []
    first, last = pl.ds(0, HALF), pl.ds(HALF, HALF)
    to_right, to_left = device(right, c, y, z), device(left, c, y, z)
    hops = []
    for k, (half, peer) in enumerate([(first, to_right), (last, to_left), (last, to_right), (first, to_left)]):
        hops.append(send(x_ref.at[half], xall.at[x, c, half], g_s.at[k], g_r.at[k], peer))
    pending += hops
    whole = send(x_ref, xall.at[x, c], c_s.at[6], c_r.at[6], partner)
    pending.append(whole)
    mine = x_ref[...]
    xall[x, c] = mine

    mine_h, mine_l = split(mine)
    mine_t = mine.T
    turned_h, turned_l = split(mine_t)
    turned = jnp.concatenate([turned_h, turned_h, turned_l], 1)

    def gram_with(high, low):
        return jnp.dot(turned, jnp.concatenate([high, low, high], 0), preferred_element_type=F32)

    lrow[...] = gram_with(mine_h, mine_l).reshape(2, 64, N)
    copies = [
        send(lrow.at[:, rows_of((y + k) % NY, 8), :], lsy.at[k - 1], ly_s.at[k - 1], ly_r.at[k - 1], peers_y[k - 1])
        for k in range(1, NY)
    ]
    total = lrow[:, rows_of(y, 8), :]
    for k, copy in enumerate(copies):
        copy.wait_recv()
        total += lsy[k]
    pending += copies
    lsz[NZ - 1] = total
    copies = [
        send(lsz.at[NZ - 1], lsz.at[k - 1], lz_s.at[k - 1], lz_r.at[k - 1], peers_z[k - 1])
        for k in range(1, NZ)
    ]

    def passed(k, source, half):
        return send(xall.at[source, c, half], xall.at[source, c, half], c_s.at[k], c_r.at[k], partner)

    hops[0].wait_recv()
    hops.append(send(xall.at[left, c, first], xall.at[left, c, first], g_s.at[4], g_r.at[4], to_right))
    hops[1].wait_recv()
    hops.append(send(xall.at[right, c, last], xall.at[right, c, last], g_s.at[5], g_r.at[5], to_left))
    on_chip = [passed(0, left, first), passed(1, right, last)]

    for copy in copies:
        copy.wait_recv()
    pending += copies
    total = jnp.zeros((2, 8, N), F32)
    for source in range(NZ):
        total += lsz[(z - source + NZ - 1) % NZ]
    own[:, rows_of(y, 8), :] = total
    copies = [
        send(own.at[:, rows_of(y, 8), :], own.at[:, rows_of(y, 8), :], la_s.at[k - 1], la_r.at[k - 1], peers_y[k - 1])
        for k in range(1, NY)
    ]
    for copy in copies:
        copy.wait_recv()
    pending += copies

    hops[2].wait_recv()
    hops[3].wait_recv()
    on_chip += [passed(2, left, last), passed(3, right, first)]

    leaf = own[...].reshape(N, N)
    (root,), (image,) = inverse_roots([leaf])
    leaves[0] = root
    leaves[1] = image
    rt[c, z, x] = leaves[:, rows_of(z, 16), :]
    copies = [
        send(rt.at[c, z, x], rt.at[c, z, x], b1_s.at[k], b1_r.at[k], peers_x[k]) for k in range(NX - 1)
    ]
    for copy in copies:
        copy.wait_recv()
    pending += copies
    copies_b = [send(rt.at[c, z], rt.at[c, z], b2_s.at[k], b2_r.at[k], peers_z[k]) for k in range(NZ - 1)]
    pending += copies_b

    hops[4].wait_recv()
    hops[5].wait_recv()
    on_chip += [passed(4, across, first), passed(5, across, last)]
    pending += hops[4:]
    pending += on_chip
    whole.wait_recv()
    for copy in on_chip:
        copy.wait_recv()

    @pl.loop(1, 5)
    def _(d):
        other = (2 * x + c - d + 8) % 8
        high, low = split(xall[other // NC, other % NC])
        part[d - 1] = gram_with(high, low).reshape(2, 64, N)

    copies = [
        send(part.at[:, :, rows_of((y + k) % NY, 8), :], rsy.at[k - 1], y_s.at[k - 1], y_r.at[k - 1], peers_y[k - 1])
        for k in range(1, NY)
    ]
    total = part[:, :, rows_of(y, 8), :]
    for k, copy in enumerate(copies):
        copy.wait_recv()
        total += rsy[k]
    pending += copies
    zsrc[...] = total.reshape(NZ, 8, N)
    copies = [
        send(zsrc.at[(z + k) % NZ], rsz.at[k - 1], z_s.at[k - 1], z_r.at[k - 1], peers_z[k - 1]) for k in range(1, NZ)
    ]
    total = zsrc[z]
    for k, copy in enumerate(copies):
        copy.wait_recv()
        total += rsz[k]
    pending += copies
    spot = rows_of(y, 8)
    kall[c, z, x, spot, :] = total
    copies = [
        send(kall.at[c, z, x, spot, :], kall.at[c, z, x, spot, :], p1_s.at[k], p1_r.at[k], peers_x[k])
        for k in range(NX - 1)
    ]
    for copy in copies:
        copy.wait_recv()
    pending += copies
    copies = [
        send(kall.at[c, z, :, spot, :], kall.at[c, z, :, spot, :], p2_s.at[k], p2_r.at[k], peers_z[k])
        for k in range(NZ - 1)
    ]
    for copy in copies:
        copy.wait_recv()
    pending += copies
    by_d = []
    for d in range(4):
        pair = pl.ds(2 * d, 2)
        by_d.append(
            [
                send(kall.at[c, pair, :, spot, :], kall.at[c, pair, :, spot, :], p3_s.at[d, k], p3_r.at[d, k], peers_y[k])
                for k in range(NY - 1)
            ]
        )
    for copy in copies_b:
        copy.wait_recv()
    swap = [send(rt.at[c], rt.at[c], b4_s, b4_r, partner)]
    for d in range(4):
        pair = pl.ds(2 * d, 2)
        for copy in by_d[d]:
            copy.wait_recv()
        pending += by_d[d]
        swap.append(send(kall.at[c, pair], kall.at[c, pair], p4_s.at[d], p4_r.at[d], partner))
    for copy in swap:
        copy.wait_recv()
    pending += swap
    for copy in pending:
        copy.wait_send()


def finish(tm_ref, xall, kall, rt, own, sk_ref, coef_ref, def_ref):
    tm = tm_ref[0]

    def at(o):
        g = (tm - o + 8) % 8
        return g // NC, g % NC

    def leaf(which, o):
        x, c = at(o)
        return rt[c, :, x, which].reshape(N, N)

    def stored(o, d):
        x, c = at(o)
        return jnp.concatenate([kall[c, 2 * d - 2, x], kall[c, 2 * d - 1, x]], 0)

    def block(a, b):
        return stored(a, b - a) if b - a <= 4 else stored(b, 8 - b + a).T

    def x_of(o):
        x, c = at(o)
        return xall[x, c]

    coef_ref[...], def_ref[...] = tree(
        functools.partial(leaf, 0),
        functools.partial(leaf, 1),
        block,
        own[...].reshape(N, N),
        lambda level: sk_ref[level],
        x_of,
    )


def body(snapshots, sketches):
    dma = pltpu.SemaphoreType.DMA
    vmem = pl.BlockSpec(memory_space=pltpu.VMEM)
    shapes = [(NX, NC, ROWS, N), (NC, NZ, NX, 64, N), (NC, NZ, NX, 2, 16, N), (2, 64, N)]
    counts = [6, 6, 7, 7, 7, 7, 7, 7, 3, 3, 7, 7, (4, 7), (4, 7), 4, 4, 7, 7, 7, 7, 7, 7, 3, 3, 7, 7]
    xall, kall, rt, own = pl.pallas_call(
        exchange,
        out_shape=[jax.ShapeDtypeStruct(s, F32) for s in shapes],
        in_specs=[vmem],
        out_specs=[vmem] * 4,
        scratch_shapes=[
            pltpu.VMEM((4, 2, 64, N), F32),
            pltpu.VMEM((NY - 1, 4, 2, 8, N), F32),
            pltpu.VMEM((NZ - 1, 8, N), F32),
            pltpu.VMEM((NZ, 8, N), F32),
            pltpu.VMEM((2, 64, N), F32),
            pltpu.VMEM((NY - 1, 2, 8, N), F32),
            pltpu.VMEM((NZ, 2, 8, N), F32),
            pltpu.VMEM((2, N, N), F32),
            *[dma(n if isinstance(n, tuple) else (n,)) for n in counts],
            dma,
            dma,
        ],
        compiler_params=pltpu.CompilerParams(collective_id=0, has_side_effects=True, vmem_limit_bytes=48 << 20),
        name="exchange",
    )(snapshots)
    tm = lax.axis_index("tm").astype(jnp.int32).reshape(1)
    return pl.pallas_call(
        finish,
        out_shape=[jax.ShapeDtypeStruct((N, N), F32), jax.ShapeDtypeStruct((ROWS, N), F32)],
        in_specs=[pl.BlockSpec(memory_space=pltpu.SMEM)] + [vmem] * 5,
        out_specs=[vmem] * 2,
        compiler_params=pltpu.CompilerParams(vmem_limit_bytes=60 << 20),
        name="finish",
    )(tm, xall, kall, rt, own, sketches)


def solution(mesh):
    placed = (P("row", "tm"), P())
    return jax.shard_map(
        body, mesh=mesh, in_specs=placed, out_specs=(P(None, "tm"), P("row", "tm")), check_vma=False
    )
```

time: 262 us -> 117 us (0.45)
  the two profiles are of different devices: /device:TPU:8 before, /device:TPU:1 now
where the time goes in v1:
time: 117 us
  Pallas kernels  112 us (96%)
  local copies, waits for them, and re-layouts  3.98 us (3%)
    pallas_call x1, Pallas kernels, body(): pl.pallas_call(exchange, out_shape=[jax.ShapeDtypeStruct(s, F32) for s in...  90.2 us
    pallas_call x1, Pallas kernels, body(): pl.pallas_call(finish, out_shape=[jax.ShapeDtypeStruct((N, N), F32), jax....  22.1 us
    unnamed x8, local copies, waits for them, and re-layouts  3.98 us

profile of v1, /device:TPU:1, one launch (start us, length us, event | category | flops | bytes accessed | tf_op | source)
XLA Modules:
  0.0 117.0 jit_solution(6070207897589732219)
XLA Ops:
  0.6 0.0 copy-start.2
  0.6 1.0 copy-done.2
  1.7 90.2 %exchange.1 = (f32[4,2,1024,128]{3,2,1,0:T(8,128)}, f32[2,8,4,64,128]{4,3,2,1,0:T(8,128)S(1)}, f32[2,8,4,2,16,128]{5,4,3,2,1,0:T(8,128)S(1)}, f32[2,64,128]{2,1,0:T(8,128)S(1)}) custom-call(f32[1024,128]{1,0:T(8,128)S(1)} %copy-done.2), custom_call_target="tpu_custom_call" | custom-call | tf_op jit(solution)/shard_map/exchange/pallas_call | solution.py:330
  91.8 0.0 copy-start
  91.9 1.3 %copy-done = f32[2,8,4,64,128]{4,3,2,1,0:T(8,128)} copy-done((f32[2,8,4,64,128]{4,3,2,1,0:T(8,128)}, f32[2,8,4,64,128]{4,3,2,1,0:T(8,128)S(1)}, u32[]{:S(2)}) %copy-start) | copy-done | bytes 2097176
  93.2 0.0 copy-start.1
  93.2 1.0 copy-done.1
  94.2 0.0 copy-start.3
  94.2 0.6 copy-done.3
  94.8 22.1 %finish.1 = (f32[128,128]{1,0:T(8,128)}, f32[1024,128]{1,0:T(8,128)}) custom-call(s32[1]{0:T(128)} %bitcast.tm_ref, f32[4,2,1024,128]{3,2,1,0:T(8,128)} %get-tuple-element.6.xall, f32[2,8,4,64,128]{4,3,2,1,0:T(8,128)} %copy-done, f32[2,8,4,2,16,128]{5,4,3,2,1,0:T(8,128)} %copy-done.1, f32[2,64,128]{2,1,0:T(8,128)} %copy-done.3, f32[3,256,128]{2,1,0:T(8,128)} %sk_ref.1), custom_call_target="tpu_custom_call" | custom-call | tf_op jit(solution)/shard_map/finish/pallas_call | solution.py:352
Async XLA Ops:
  0.6 1.0 copy-start.2
  91.8 1.3 %copy-start = (f32[2,8,4,64,128]{4,3,2,1,0:T(8,128)}, f32[2,8,4,64,128]{4,3,2,1,0:T(8,128)S(1)}, u32[]{:S(2)}) copy-start(f32[2,8,4,64,128]{4,3,2,1,0:T(8,128)S(1)} %get-tuple-element.7.kall) | copy-start | bytes 6291460
  93.2 1.0 copy-start.1
  94.2 0.6 copy-start.3

commit v2 on v1

--- a/solution.py
+++ b/solution.py
@@ -59,7 +59,8 @@
     return s, mm(s.T, mm(gram, s))
 
 
-def tree(root, image, block, own, sketch, x_of):
+def tree(root, image, block, own, sketch, x_of, gate):
+    gate(0)
     r = [root(o) for o in range(8)]
     s0, a0, e0 = [], [], []
     for j in range(4):
@@ -69,12 +70,15 @@
         a0.append(a)
     for j in range(4):
         e0.append(jnp.concatenate([mm(r[2 * j + 1], s0[j][:N]), mm(r[2 * j], s0[j][N:])], 0))
+    gate(1)
+    gate(2)
     cross1 = []
     for j in range(0, 4, 2):
         upper = jnp.concatenate([block(2 * j + 1, 2 * j + 3), block(2 * j + 1, 2 * j + 2)], 1)
         lower = jnp.concatenate([block(2 * j, 2 * j + 3), block(2 * j, 2 * j + 2)], 1)
         cross1.append(mm(e0[j].T, mm(jnp.concatenate([upper, lower], 0), e0[j + 1])))
     r1, t1 = inverse_roots(a0)
+    gate(3)
     s1, a1, e1 = [], [], []
     for j in range(2):
         cross = mm(mm(r1[2 * j], cross1[j]), r1[2 * j + 1])
@@ -104,10 +108,13 @@
 
 def place():
     tm, row = lax.axis_index("tm"), lax.axis_index("row")
-    return tm // NC, tm % NC, row % NY, row // NY
-
-
-def device(x, c, y, z):
+    c = tm % NC
+    y, z = row % NY, row // NY
+    return tm // NC, c, y + c * (z - y), z + c * (y - z)
+
+
+def device(x, c, core, u, v):
+    y, z = u + core * (v - u), v + core * (u - v)
     return (x * NC + c, z * NY + y)
 
 
@@ -115,20 +122,35 @@
     return pl.ds(pl.multiple_of(index * count, count), count)
 
 
-def exchange(x_ref, xall, kall, rt, own, part, rsy, rsz, zsrc, lrow, lsy, lsz, leaves,
+def step(x_hbm, sk_ref, coef_ref, def_ref, x_ref, xall, kall, rt, own, part, rsy, rsz, zsrc, lrow, lsy, lsz, leaves,
              g_s, g_r, c_s, c_r, y_s, y_r, z_s, z_r, p1_s, p1_r, p2_s, p2_r, p3_s, p3_r, p4_s, p4_r,
-             ly_s, ly_r, lz_s, lz_r, la_s, la_r, b1_s, b1_r, b2_s, b2_r, b4_s, b4_r):
-    x, c, y, z = place()
+             ly_s, ly_r, lz_s, lz_r, la_s, la_r, b1_s, b1_r, b2_s, b2_r, b4_s, b4_r, load_s):
+    x, c, u, v = place()
+    tm = x * NC + c
     left, right, across = (x + 3) % NX, (x + 1) % NX, (x + 2) % NX
-    peers_x = [device((x + k) % NX, c, y, z) for k in range(1, NX)]
-    peers_y = [device(x, c, (y + k) % NY, z) for k in range(1, NY)]
-    peers_z = [device(x, c, y, (z + k) % NZ) for k in range(1, NZ)]
-    partner = device(x, 1 - c, y, z)
+    peers_x = [device((x + k) % NX, c, c, u, v) for k in range(1, NX)]
+    peers_y = [device(x, c, c, (u + k) % NY, v) for k in range(1, NY)]
+    peers_z = [device(x, c, c, u, (v + k) % NZ) for k in range(1, NZ)]
+    partner = device(x, 1 - c, c, u, v)
 
     barrier = pltpu.get_barrier_semaphore()
     everyone = peers_x + peers_y + peers_z + [partner]
     for peer in everyone:
         pl.semaphore_signal(barrier, inc=1, device_id=peer, device_id_type=MESH)
+    load = pltpu.make_async_copy(x_hbm, x_ref, load_s)
+    load.start()
+    load.wait()
+
+    mine = x_ref[...]
+    xall[x, c] = mine
+    mine_h, mine_l = split(mine)
+    turned_h, turned_l = split(mine.T)
+    turned = jnp.concatenate([turned_h, turned_h, turned_l], 1)
+
+    def gram_with(high, low):
+        return jnp.dot(turned, jnp.concatenate([high, low, high], 0), preferred_element_type=F32)
+
+    lrow[...] = gram_with(mine_h, mine_l).reshape(2, 64, N)
     pl.semaphore_wait(barrier, len(everyone))
 
     def send(src, dst, s, r, peer):
@@ -140,30 +162,18 @@
 
     pending = []
     first, last = pl.ds(0, HALF), pl.ds(HALF, HALF)
-    to_right, to_left = device(right, c, y, z), device(left, c, y, z)
+    to_right, to_left = device(right, c, c, u, v), device(left, c, c, u, v)
     hops = []
     for k, (half, peer) in enumerate([(first, to_right), (last, to_left), (last, to_right), (first, to_left)]):
         hops.append(send(x_ref.at[half], xall.at[x, c, half], g_s.at[k], g_r.at[k], peer))
     pending += hops
     whole = send(x_ref, xall.at[x, c], c_s.at[6], c_r.at[6], partner)
     pending.append(whole)
-    mine = x_ref[...]
-    xall[x, c] = mine
-
-    mine_h, mine_l = split(mine)
-    mine_t = mine.T
-    turned_h, turned_l = split(mine_t)
-    turned = jnp.concatenate([turned_h, turned_h, turned_l], 1)
-
-    def gram_with(high, low):
-        return jnp.dot(turned, jnp.concatenate([high, low, high], 0), preferred_element_type=F32)
-
-    lrow[...] = gram_with(mine_h, mine_l).reshape(2, 64, N)
-    copies = [
-        send(lrow.at[:, rows_of((y + k) % NY, 8), :], lsy.at[k - 1], ly_s.at[k - 1], ly_r.at[k - 1], peers_y[k - 1])
+    copies = [
+        send(lrow.at[:, rows_of((u + k) % NY, 8), :], lsy.at[k - 1], ly_s.at[k - 1], ly_r.at[k - 1], peers_y[k - 1])
         for k in range(1, NY)
     ]
-    total = lrow[:, rows_of(y, 8), :]
+    total = lrow[:, rows_of(u, 8), :]
     for k, copy in enumerate(copies):
         copy.wait_recv()
         total += lsy[k]
@@ -188,10 +198,10 @@
     pending += copies
     total = jnp.zeros((2, 8, N), F32)
     for source in range(NZ):
-        total += lsz[(z - source + NZ - 1) % NZ]
-    own[:, rows_of(y, 8), :] = total
-    copies = [
-        send(own.at[:, rows_of(y, 8), :], own.at[:, rows_of(y, 8), :], la_s.at[k - 1], la_r.at[k - 1], peers_y[k - 1])
+        total += lsz[(v - source + NZ - 1) % NZ]
+    own[:, rows_of(u, 8), :] = total
+    copies = [
+        send(own.at[:, rows_of(u, 8), :], own.at[:, rows_of(u, 8), :], la_s.at[k - 1], la_r.at[k - 1], peers_y[k - 1])
         for k in range(1, NY)
     ]
     for copy in copies:
@@ -206,14 +216,14 @@
     (root,), (image,) = inverse_roots([leaf])
     leaves[0] = root
     leaves[1] = image
-    rt[c, z, x] = leaves[:, rows_of(z, 16), :]
-    copies = [
-        send(rt.at[c, z, x], rt.at[c, z, x], b1_s.at[k], b1_r.at[k], peers_x[k]) for k in range(NX - 1)
-    ]
-    for copy in copies:
-        copy.wait_recv()
-    pending += copies
-    copies_b = [send(rt.at[c, z], rt.at[c, z], b2_s.at[k], b2_r.at[k], peers_z[k]) for k in range(NZ - 1)]
+    rt[c, v, x] = leaves[:, rows_of(v, 16), :]
+    copies = [
+        send(rt.at[c, v, x], rt.at[c, v, x], b1_s.at[k], b1_r.at[k], peers_x[k]) for k in range(NX - 1)
+    ]
+    for copy in copies:
+        copy.wait_recv()
+    pending += copies
+    copies_b = [send(rt.at[c, v], rt.at[c, v], b2_s.at[k], b2_r.at[k], peers_z[k]) for k in range(NZ - 1)]
     pending += copies_b
 
     hops[4].wait_recv()
@@ -232,34 +242,34 @@
         part[d - 1] = gram_with(high, low).reshape(2, 64, N)
 
     copies = [
-        send(part.at[:, :, rows_of((y + k) % NY, 8), :], rsy.at[k - 1], y_s.at[k - 1], y_r.at[k - 1], peers_y[k - 1])
+        send(part.at[:, :, rows_of((u + k) % NY, 8), :], rsy.at[k - 1], y_s.at[k - 1], y_r.at[k - 1], peers_y[k - 1])
         for k in range(1, NY)
     ]
-    total = part[:, :, rows_of(y, 8), :]
+    total = part[:, :, rows_of(u, 8), :]
     for k, copy in enumerate(copies):
         copy.wait_recv()
         total += rsy[k]
     pending += copies
     zsrc[...] = total.reshape(NZ, 8, N)
     copies = [
-        send(zsrc.at[(z + k) % NZ], rsz.at[k - 1], z_s.at[k - 1], z_r.at[k - 1], peers_z[k - 1]) for k in range(1, NZ)
-    ]
-    total = zsrc[z]
+        send(zsrc.at[(v + k) % NZ], rsz.at[k - 1], z_s.at[k - 1], z_r.at[k - 1], peers_z[k - 1]) for k in range(1, NZ)
+    ]
+    total = zsrc[v]
     for k, copy in enumerate(copies):
         copy.wait_recv()
         total += rsz[k]
     pending += copies
-    spot = rows_of(y, 8)
-    kall[c, z, x, spot, :] = total
-    copies = [
-        send(kall.at[c, z, x, spot, :], kall.at[c, z, x, spot, :], p1_s.at[k], p1_r.at[k], peers_x[k])
+    spot = rows_of(u, 8)
+    kall[c, v, x, spot, :] = total
+    copies = [
+        send(kall.at[c, v, x, spot, :], kall.at[c, v, x, spot, :], p1_s.at[k], p1_r.at[k], peers_x[k])
         for k in range(NX - 1)
     ]
     for copy in copies:
         copy.wait_recv()
     pending += copies
     copies = [
-        send(kall.at[c, z, :, spot, :], kall.at[c, z, :, spot, :], p2_s.at[k], p2_r.at[k], peers_z[k])
+        send(kall.at[c, v, :, spot, :], kall.at[c, v, :, spot, :], p2_s.at[k], p2_r.at[k], peers_z[k])
         for k in range(NZ - 1)
     ]
     for copy in copies:
@@ -276,41 +286,38 @@
         )
     for copy in copies_b:
         copy.wait_recv()
-    swap = [send(rt.at[c], rt.at[c], b4_s, b4_r, partner)]
-    for d in range(4):
+    swap = send(rt.at[c], rt.at[c], b4_s, b4_r, partner)
+    pending.append(swap)
+
+    def gate(d):
         pair = pl.ds(2 * d, 2)
         for copy in by_d[d]:
             copy.wait_recv()
-        pending += by_d[d]
-        swap.append(send(kall.at[c, pair], kall.at[c, pair], p4_s.at[d], p4_r.at[d], partner))
-    for copy in swap:
-        copy.wait_recv()
-    pending += swap
-    for copy in pending:
-        copy.wait_send()
-
-
-def finish(tm_ref, xall, kall, rt, own, sk_ref, coef_ref, def_ref):
-    tm = tm_ref[0]
+        over = send(kall.at[c, pair], kall.at[c, pair], p4_s.at[d], p4_r.at[d], partner)
+        if d == 0:
+            swap.wait_recv()
+        over.wait_recv()
+        pending.append(over)
+        pending.extend(by_d[d])
 
     def at(o):
         g = (tm - o + 8) % 8
         return g // NC, g % NC
 
     def leaf(which, o):
-        x, c = at(o)
-        return rt[c, :, x, which].reshape(N, N)
+        gx, gc = at(o)
+        return rt[gc, :, gx, which].reshape(N, N)
 
     def stored(o, d):
-        x, c = at(o)
-        return jnp.concatenate([kall[c, 2 * d - 2, x], kall[c, 2 * d - 1, x]], 0)
+        gx, gc = at(o)
+        return jnp.concatenate([kall[gc, 2 * d - 2, gx], kall[gc, 2 * d - 1, gx]], 0)
 
     def block(a, b):
         return stored(a, b - a) if b - a <= 4 else stored(b, 8 - b + a).T
 
     def x_of(o):
-        x, c = at(o)
-        return xall[x, c]
+        gx, gc = at(o)
+        return xall[gx, gc]
 
     coef_ref[...], def_ref[...] = tree(
         functools.partial(leaf, 0),
@@ -319,44 +326,46 @@
         own[...].reshape(N, N),
         lambda level: sk_ref[level],
         x_of,
+        gate,
     )
+    for copy in pending:
+        copy.wait_send()
 
 
 def body(snapshots, sketches):
     dma = pltpu.SemaphoreType.DMA
     vmem = pl.BlockSpec(memory_space=pltpu.VMEM)
-    shapes = [(NX, NC, ROWS, N), (NC, NZ, NX, 64, N), (NC, NZ, NX, 2, 16, N), (2, 64, N)]
     counts = [6, 6, 7, 7, 7, 7, 7, 7, 3, 3, 7, 7, (4, 7), (4, 7), 4, 4, 7, 7, 7, 7, 7, 7, 3, 3, 7, 7]
-    xall, kall, rt, own = pl.pallas_call(
-        exchange,
-        out_shape=[jax.ShapeDtypeStruct(s, F32) for s in shapes],
-        in_specs=[vmem],
-        out_specs=[vmem] * 4,
+    shapes = [
+        (ROWS, N),
+        (NX, NC, ROWS, N),
+        (NC, NZ, NX, 64, N),
+        (NC, NZ, NX, 2, 16, N),
+        (2, 64, N),
+        (4, 2, 64, N),
+        (NY - 1, 4, 2, 8, N),
+        (NZ - 1, 8, N),
+        (NZ, 8, N),
+        (2, 64, N),
+        (NY - 1, 2, 8, N),
+        (NZ, 2, 8, N),
+        (2, N, N),
+    ]
+    return pl.pallas_call(
+        step,
+        out_shape=[jax.ShapeDtypeStruct((N, N), F32), jax.ShapeDtypeStruct((ROWS, N), F32)],
+        in_specs=[pl.BlockSpec(memory_space=pl.ANY), vmem],
+        out_specs=[vmem] * 2,
         scratch_shapes=[
-            pltpu.VMEM((4, 2, 64, N), F32),
-            pltpu.VMEM((NY - 1, 4, 2, 8, N), F32),
-            pltpu.VMEM((NZ - 1, 8, N), F32),
-            pltpu.VMEM((NZ, 8, N), F32),
-            pltpu.VMEM((2, 64, N), F32),
-            pltpu.VMEM((NY - 1, 2, 8, N), F32),
-            pltpu.VMEM((NZ, 2, 8, N), F32),
-            pltpu.VMEM((2, N, N), F32),
+            *[pltpu.VMEM(s, F32) for s in shapes],
             *[dma(n if isinstance(n, tuple) else (n,)) for n in counts],
             dma,
             dma,
+            dma,
         ],
-        compiler_params=pltpu.CompilerParams(collective_id=0, has_side_effects=True, vmem_limit_bytes=48 << 20),
-        name="exchange",
-    )(snapshots)
-    tm = lax.axis_index("tm").astype(jnp.int32).reshape(1)
-    return pl.pallas_call(
-        finish,
-        out_shape=[jax.ShapeDtypeStruct((N, N), F32), jax.ShapeDtypeStruct((ROWS, N), F32)],
-        in_specs=[pl.BlockSpec(memory_space=pltpu.SMEM)] + [vmem] * 5,
-        out_specs=[vmem] * 2,
-        compiler_params=pltpu.CompilerParams(vmem_limit_bytes=60 << 20),
-        name="finish",
-    )(tm, xall, kall, rt, own, sketches)
+        compiler_params=pltpu.CompilerParams(collective_id=0, has_side_effects=True, vmem_limit_bytes=60 << 20),
+        name="step",
+    )(snapshots, sketches)
 
 
 def solution(mesh):

time: 117 us -> 97.4 us (0.83)
  Pallas kernels: 112 us -> 93.2 us
    pallas_call x2 -> x1, Pallas kernels: 112 us -> 93.2 us  [body(): pl.pallas_call(step, out_shape=[jax.ShapeDtypeStruct((N, N), F32), jax.Sh...]
    unnamed x8 -> x2, local copies, waits for them, and re-layouts: 3.98 us -> 3.34 us
where the time goes in v2:
time: 97.4 us; the launch traced here: 97.1 us
  Pallas kernels  93.2 us (96%)
  local copies, waits for them, and re-layouts  3.34 us (3%)
    pallas_call x1, Pallas kernels, body(): pl.pallas_call(step, out_shape=[jax.ShapeDtypeStruct((N, N), F32), jax.Sh...  93.2 us
    unnamed x2, local copies, waits for them, and re-layouts  3.34 us

profile of v2, /device:TPU:1, one launch (start us, length us, event | category | flops | bytes accessed | tf_op | source)
XLA Modules:
  0.0 97.1 jit_solution(2588108930695563997)
XLA Ops:
  0.6 93.2 %step.1 = (f32[128,128]{1,0:T(8,128)}, f32[1024,128]{1,0:T(8,128)}) custom-call(f32[1024,128]{1,0:T(8,128)} %x_hbm.1, f32[3,256,128]{2,1,0:T(8,128)} %sk_ref.1), custom_call_target="tpu_custom_call" | custom-call | tf_op jit(solution)/shard_map/step/pallas_call | solution.py:354
  93.8 1.5 %copy.6 = f32[128,128]{1,0:T(8,128)} copy(f32[128,128]{1,0:T(8,128)} %get-tuple-element.4) | data formatting | bytes 131072
  95.3 1.9 %copy.7 = f32[1024,128]{1,0:T(8,128)} copy(f32[1024,128]{1,0:T(8,128)} %get-tuple-element.5) | data formatting | bytes 1048576

commit v3 on v2

--- a/solution.py
+++ b/solution.py
@@ -12,7 +12,7 @@
 NX, NC, NY, NZ = 4, 2, 8, 8
 N = 128
 ROWS = 1024
-HALF = ROWS // 2
+SPLIT = 384
 
 
 def split(a):
@@ -102,8 +102,8 @@
     x_all = jnp.concatenate([x_of(o) for o in range(7, -1, -1)], 1)
     base = mm(x_all, jnp.concatenate([upper, lower], 0))
     r3 = inverse_roots([a2], False)[0][0]
-    coefficients = mm(h, r3).T
-    return coefficients, x_of(0) - mm(base, mm(r3, coefficients))
+    turned = mm(h, r3)
+    return turned, mm(base, mm(r3, turned.T))
 
 
 def place():
@@ -161,12 +161,24 @@
         return copy
 
     pending = []
-    first, last = pl.ds(0, HALF), pl.ds(HALF, HALF)
+    first, last = pl.ds(0, SPLIT), pl.ds(SPLIT, ROWS - SPLIT)
     to_right, to_left = device(right, c, c, u, v), device(left, c, c, u, v)
-    hops = []
-    for k, (half, peer) in enumerate([(first, to_right), (last, to_left), (last, to_right), (first, to_left)]):
-        hops.append(send(x_ref.at[half], xall.at[x, c, half], g_s.at[k], g_r.at[k], peer))
-    pending += hops
+
+    def hop(k, source, part_of, peer, src=None):
+        src = xall.at[source, c, part_of] if src is None else src
+        copy = send(src, xall.at[source, c, part_of], g_s.at[k], g_r.at[k], peer)
+        pending.append(copy)
+        return copy
+
+    def passed(k, source, part_of):
+        here = xall.at[source, c, part_of]
+        copy = send(here, here, c_s.at[k], c_r.at[k], partner)
+        pending.append(copy)
+        return copy
+
+    hop0 = hop(0, x, first, to_right, x_ref.at[first])
+    hop1 = hop(1, x, last, to_left, x_ref.at[last])
+    hop2 = hop(2, x, last, to_right, x_ref.at[last])
     whole = send(x_ref, xall.at[x, c], c_s.at[6], c_r.at[6], partner)
     pending.append(whole)
     copies = [
@@ -184,14 +196,9 @@
         for k in range(1, NZ)
     ]
 
-    def passed(k, source, half):
-        return send(xall.at[source, c, half], xall.at[source, c, half], c_s.at[k], c_r.at[k], partner)
-
-    hops[0].wait_recv()
-    hops.append(send(xall.at[left, c, first], xall.at[left, c, first], g_s.at[4], g_r.at[4], to_right))
-    hops[1].wait_recv()
-    hops.append(send(xall.at[right, c, last], xall.at[right, c, last], g_s.at[5], g_r.at[5], to_left))
-    on_chip = [passed(0, left, first), passed(1, right, last)]
+    hop0.wait_recv()
+    hop4 = hop(4, left, first, to_right)
+    chip0 = passed(0, left, first)
 
     for copy in copies:
         copy.wait_recv()
@@ -204,52 +211,71 @@
         send(own.at[:, rows_of(u, 8), :], own.at[:, rows_of(u, 8), :], la_s.at[k - 1], la_r.at[k - 1], peers_y[k - 1])
         for k in range(1, NY)
     ]
+    hop1.wait_recv()
+    hop5 = hop(5, right, last, to_left)
+    hop3 = hop(3, x, first, to_left, x_ref.at[first])
+    chip1 = passed(1, right, last)
     for copy in copies:
         copy.wait_recv()
     pending += copies
-
-    hops[2].wait_recv()
-    hops[3].wait_recv()
-    on_chip += [passed(2, left, last), passed(3, right, first)]
 
     leaf = own[...].reshape(N, N)
     (root,), (image,) = inverse_roots([leaf])
     leaves[0] = root
     leaves[1] = image
     rt[c, v, x] = leaves[:, rows_of(v, 16), :]
-    copies = [
+    copies_x = [
         send(rt.at[c, v, x], rt.at[c, v, x], b1_s.at[k], b1_r.at[k], peers_x[k]) for k in range(NX - 1)
     ]
-    for copy in copies:
-        copy.wait_recv()
-    pending += copies
-    copies_b = [send(rt.at[c, v], rt.at[c, v], b2_s.at[k], b2_r.at[k], peers_z[k]) for k in range(NZ - 1)]
-    pending += copies_b
-
-    hops[4].wait_recv()
-    hops[5].wait_recv()
-    on_chip += [passed(4, across, first), passed(5, across, last)]
-    pending += hops[4:]
-    pending += on_chip
-    whole.wait_recv()
-    for copy in on_chip:
-        copy.wait_recv()
-
-    @pl.loop(1, 5)
-    def _(d):
+    pending += copies_x
+    hop2.wait_recv()
+    chip2 = passed(2, left, last)
+
+    def cross_gram(d):
         other = (2 * x + c - d + 8) % 8
         high, low = split(xall[other // NC, other % NC])
         part[d - 1] = gram_with(high, low).reshape(2, 64, N)
 
-    copies = [
-        send(part.at[:, :, rows_of((u + k) % NY, 8), :], rsy.at[k - 1], y_s.at[k - 1], y_r.at[k - 1], peers_y[k - 1])
-        for k in range(1, NY)
-    ]
+    def first_sum(half):
+        pair = pl.ds(2 * half, 2)
+        return [
+            send(
+                part.at[pair, :, rows_of((u + k) % NY, 8), :],
+                rsy.at[k - 1, pair],
+                y_s.at[half, k - 1],
+                y_r.at[half, k - 1],
+                peers_y[k - 1],
+            )
+            for k in range(1, NY)
+        ]
+
+    whole.wait_recv()
+    chip0.wait_recv()
+    chip2.wait_recv()
+    cross_gram(1)
+    cross_gram(2)
+    sums = [first_sum(0)]
+    hop4.wait_recv()
+    chip4 = passed(4, across, first)
+    hop5.wait_recv()
+    chip5 = passed(5, across, last)
+    for copy in copies_x:
+        copy.wait_recv()
+    copies_b = [send(rt.at[c, v], rt.at[c, v], b2_s.at[k], b2_r.at[k], peers_z[k]) for k in range(NZ - 1)]
+    pending += copies_b
+    chip4.wait_recv()
+    chip5.wait_recv()
+    cross_gram(3)
+    cross_gram(4)
+    sums.append(first_sum(1))
+    hop3.wait_recv()
+    chip3 = passed(3, right, first)
+    pending += sums[0] + sums[1]
     total = part[:, :, rows_of(u, 8), :]
-    for k, copy in enumerate(copies):
-        copy.wait_recv()
+    for k in range(NY - 1):
+        sums[0][k].wait_recv()
+        sums[1][k].wait_recv()
         total += rsy[k]
-    pending += copies
     zsrc[...] = total.reshape(NZ, 8, N)
     copies = [
         send(zsrc.at[(v + k) % NZ], rsz.at[k - 1], z_s.at[k - 1], z_r.at[k - 1], peers_z[k - 1]) for k in range(1, NZ)
@@ -296,6 +322,9 @@
         over = send(kall.at[c, pair], kall.at[c, pair], p4_s.at[d], p4_r.at[d], partner)
         if d == 0:
             swap.wait_recv()
+        if d == 3:
+            chip1.wait_recv()
+            chip3.wait_recv()
         over.wait_recv()
         pending.append(over)
         pending.extend(by_d[d])
@@ -335,7 +364,7 @@
 def body(snapshots, sketches):
     dma = pltpu.SemaphoreType.DMA
     vmem = pl.BlockSpec(memory_space=pltpu.VMEM)
-    counts = [6, 6, 7, 7, 7, 7, 7, 7, 3, 3, 7, 7, (4, 7), (4, 7), 4, 4, 7, 7, 7, 7, 7, 7, 3, 3, 7, 7]
+    counts = [6, 6, 7, 7, (2, 7), (2, 7), 7, 7, 3, 3, 7, 7, (4, 7), (4, 7), 4, 4, 7, 7, 7, 7, 7, 7, 3, 3, 7, 7]
     shapes = [
         (ROWS, N),
         (NX, NC, ROWS, N),
@@ -351,7 +380,7 @@
         (NZ, 2, 8, N),
         (2, N, N),
     ]
-    return pl.pallas_call(
+    turned, removed = pl.pallas_call(
         step,
         out_shape=[jax.ShapeDtypeStruct((N, N), F32), jax.ShapeDtypeStruct((ROWS, N), F32)],
         in_specs=[pl.BlockSpec(memory_space=pl.ANY), vmem],
@@ -366,6 +395,7 @@
         compiler_params=pltpu.CompilerParams(collective_id=0, has_side_effects=True, vmem_limit_bytes=60 << 20),
         name="step",
     )(snapshots, sketches)
+    return turned.T, snapshots - removed
 
 
 def solution(mesh):

time: 97.4 us -> 99.9 us (1.026)
  Pallas kernels: 93.2 us -> 95.6 us
  other arithmetic: 0 us -> 1.89 us
  local copies, waits for them, and re-layouts: 3.34 us -> 1.57 us
    pallas_call x1, Pallas kernels: 93.2 us -> 95.6 us  [body(): pl.pallas_call(step, out_shape=[jax.ShapeDtypeStruct((N, N), F32), jax.Sh...]
    sub x0 -> x1, other arithmetic: none -> 1.89 us  [body(): return (turned.T, snapshots - removed)]
    unnamed x2 -> x3, local copies, waits for them, and re-layouts: 3.34 us -> 1.57 us
where the time goes in v3:
time: 99.9 us; the launch traced here: 99.7 us
  Pallas kernels  95.6 us (96%)
  other arithmetic  1.89 us (2%)
  local copies, waits for them, and re-layouts  1.57 us (2%)
    pallas_call x1, Pallas kernels, body(): pl.pallas_call(step, out_shape=[jax.ShapeDtypeStruct((N, N), F32), jax.Sh...  95.6 us

profile of v3, /device:TPU:1, one launch (start us, length us, event | category | flops | bytes accessed | tf_op | source)
XLA Modules:
  0.0 99.7 jit_solution(6927643538206488423)
XLA Ops:
  0.6 0.0 copy-start
  0.6 95.6 %step.1 = (f32[128,128]{1,0:T(8,128)}, f32[1024,128]{1,0:T(8,128)}) custom-call(f32[1024,128]{1,0:T(8,128)} %x_hbm.1, f32[3,256,128]{2,1,0:T(8,128)} %sk_ref.1), custom_call_target="tpu_custom_call" | custom-call | tf_op jit(solution)/shard_map/step/pallas_call | solution.py:383
  96.2 1.6 %copy.4 = f32[128,128]{1,0:T(8,128)} copy(f32[128,128]{0,1:T(8,128)} %bitcast.1) | data formatting | bytes 131072
  97.8 0.0 copy-done
  97.8 1.9 %sub.3 = f32[1024,128]{1,0:T(8,128)} subtract(f32[1024,128]{1,0:T(8,128)S(1)} %copy-done, f32[1024,128]{1,0:T(8,128)} %get-tuple-element.5) | non-fusion elementwise | flops 131072 | bytes 1572864 | tf_op jit(solution)/shard_map/sub | solution.py:398
Async XLA Ops:
  0.6 97.1 %copy-start = (f32[1024,128]{1,0:T(8,128)S(1)}, f32[1024,128]{1,0:T(8,128)}, u32[]{:S(2)}) copy-start(f32[1024,128]{1,0:T(8,128)} %x_hbm.1) | copy-start | bytes 1572868

commit v4 on v3

--- a/solution.py
+++ b/solution.py
@@ -1,5 +1,3 @@
-import functools
-
 import jax
 import jax.numpy as jnp
 from jax import lax
@@ -70,6 +68,7 @@
         a0.append(a)
     for j in range(4):
         e0.append(jnp.concatenate([mm(r[2 * j + 1], s0[j][:N]), mm(r[2 * j], s0[j][N:])], 0))
+    r1, t1 = inverse_roots(a0)
     gate(1)
     gate(2)
     cross1 = []
@@ -77,8 +76,6 @@
         upper = jnp.concatenate([block(2 * j + 1, 2 * j + 3), block(2 * j + 1, 2 * j + 2)], 1)
         lower = jnp.concatenate([block(2 * j, 2 * j + 3), block(2 * j, 2 * j + 2)], 1)
         cross1.append(mm(e0[j].T, mm(jnp.concatenate([upper, lower], 0), e0[j + 1])))
-    r1, t1 = inverse_roots(a0)
-    gate(3)
     s1, a1, e1 = [], [], []
     for j in range(2):
         cross = mm(mm(r1[2 * j], cross1[j]), r1[2 * j + 1])
@@ -89,12 +86,13 @@
         upper = mm(e0[2 * j + 1], mm(r1[2 * j + 1], s1[j][:N]))
         lower = mm(e0[2 * j], mm(r1[2 * j], s1[j][N:]))
         e1.append(jnp.concatenate([upper, lower], 0))
+    r2, t2 = inverse_roots(a1)
+    gate(3)
     wide = [jnp.concatenate([block(a, b) for b in (7, 6, 5, 4)], 1) for a in (3, 2, 1, 0)]
     cross2 = mm(e1[0].T, mm(jnp.concatenate(wide, 0), e1[1]))
     near = jnp.concatenate([block(0, 3), block(0, 2), block(0, 1), own], 1)
     far = jnp.concatenate([block(0, 7), block(0, 6), block(0, 5), block(0, 4)], 1)
     w_far, w_near = mm(far, e1[1]), mm(near, e1[0])
-    r2, t2 = inverse_roots(a1)
     s2, a2 = sketched(t2[1], t2[0], mm(mm(r2[0], cross2), r2[1]), sketch(2))
     h = mm(jnp.concatenate([mm(w_far, r2[1]), mm(w_near, r2[0])], 1), s2)
     upper = mm(e1[1], mm(r2[1], s2[:N]))
@@ -122,9 +120,9 @@
     return pl.ds(pl.multiple_of(index * count, count), count)
 
 
-def step(x_hbm, sk_ref, coef_ref, def_ref, x_ref, xall, kall, rt, own, part, rsy, rsz, zsrc, lrow, lsy, lsz, leaves,
-             g_s, g_r, c_s, c_r, y_s, y_r, z_s, z_r, p1_s, p1_r, p2_s, p2_r, p3_s, p3_r, p4_s, p4_r,
-             ly_s, ly_r, lz_s, lz_r, la_s, la_r, b1_s, b1_r, b2_s, b2_r, b4_s, b4_r, load_s):
+def step(x_hbm, sk_ref, coef_ref, def_ref, x_ref, xall, kall, leaves, roots, part, rsy, rsz, lrow, lsy, lsz,
+         g_s, g_r, c_s, c_r, y_s, y_r, z_s, z_r, p1_s, p1_r, p3_s, p3_r, p4_s, p4_r,
+         ly_s, ly_r, lz_s, lz_r, b1_s, b1_r, b2_s, b2_r, b4_s, b4_r, load_s):
     x, c, u, v = place()
     tm = x * NC + c
     left, right, across = (x + 3) % NX, (x + 1) % NX, (x + 2) % NX
@@ -200,34 +198,32 @@
     hop4 = hop(4, left, first, to_right)
     chip0 = passed(0, left, first)
 
-    for copy in copies:
-        copy.wait_recv()
-    pending += copies
-    total = jnp.zeros((2, 8, N), F32)
-    for source in range(NZ):
-        total += lsz[(v - source + NZ - 1) % NZ]
-    own[:, rows_of(u, 8), :] = total
-    copies = [
-        send(own.at[:, rows_of(u, 8), :], own.at[:, rows_of(u, 8), :], la_s.at[k - 1], la_r.at[k - 1], peers_y[k - 1])
-        for k in range(1, NY)
-    ]
+    def in_order(slots):
+        total = slots[(v + NZ - 1) % NZ]
+        for source in range(1, NZ):
+            total += slots[(v - source + NZ - 1) % NZ]
+        return total
+
+    def received(copies):
+        for copy in copies:
+            copy.wait_recv()
+        pending.extend(copies)
+
+    spot = rows_of(u, 8)
+
+    def to_line(src, dst, s, r, peers):
+        return [send(src, dst, s.at[k], r.at[k], peer) for k, peer in enumerate(peers)]
+
+    def same(ref, s, r, peers):
+        return to_line(ref, ref, s, r, peers)
+
+    received(copies)
+    leaves[c, :, x, spot, :] = in_order(lsz)
+    leaf_x = same(leaves.at[c, :, x, spot, :], b1_s, b1_r, peers_x)
     hop1.wait_recv()
     hop5 = hop(5, right, last, to_left)
     hop3 = hop(3, x, first, to_left, x_ref.at[first])
     chip1 = passed(1, right, last)
-    for copy in copies:
-        copy.wait_recv()
-    pending += copies
-
-    leaf = own[...].reshape(N, N)
-    (root,), (image,) = inverse_roots([leaf])
-    leaves[0] = root
-    leaves[1] = image
-    rt[c, v, x] = leaves[:, rows_of(v, 16), :]
-    copies_x = [
-        send(rt.at[c, v, x], rt.at[c, v, x], b1_s.at[k], b1_r.at[k], peers_x[k]) for k in range(NX - 1)
-    ]
-    pending += copies_x
     hop2.wait_recv()
     chip2 = passed(2, left, last)
 
@@ -236,12 +232,12 @@
         high, low = split(xall[other // NC, other % NC])
         part[d - 1] = gram_with(high, low).reshape(2, 64, N)
 
-    def first_sum(half):
+    def scatter(half):
         pair = pl.ds(2 * half, 2)
         return [
             send(
                 part.at[pair, :, rows_of((u + k) % NY, 8), :],
-                rsy.at[k - 1, pair],
+                rsy.at[half, k - 1],
                 y_s.at[half, k - 1],
                 y_r.at[half, k - 1],
                 peers_y[k - 1],
@@ -249,93 +245,90 @@
             for k in range(1, NY)
         ]
 
+    def spread(half, copies):
+        received(copies)
+        total = part[2 * half : 2 * half + 2, :, spot, :]
+        for k in range(NY - 1):
+            total += rsy[half, k]
+        rsz[half, NZ - 1] = total.reshape(4, 8, N)
+        return [
+            send(rsz.at[half, NZ - 1], rsz.at[half, k], z_s.at[half, k], z_r.at[half, k], peers_z[k])
+            for k in range(NZ - 1)
+        ]
+
+    def along_x(half, copies):
+        received(copies)
+        quad = pl.ds(4 * half, 4)
+        kall[c, quad, x, spot, :] = in_order(rsz.at[half])
+        return same(kall.at[c, quad, x, spot, :], p1_s.at[half], p1_r.at[half], peers_x)
+
+    def along_u(half, copies):
+        received(copies)
+        return [
+            same(kall.at[c, pl.ds(2 * d, 2), :, spot, :], p3_s.at[d], p3_r.at[d], peers_y)
+            for d in (2 * half, 2 * half + 1)
+        ]
+
+    def swap(d, copies):
+        received(copies)
+        pair = pl.ds(2 * d, 2)
+        over = send(kall.at[c, pair], kall.at[c, pair], p4_s.at[d], p4_r.at[d], partner)
+        pending.append(over)
+        return over
+
     whole.wait_recv()
     chip0.wait_recv()
     chip2.wait_recv()
     cross_gram(1)
     cross_gram(2)
-    sums = [first_sum(0)]
+    near = scatter(0)
     hop4.wait_recv()
     chip4 = passed(4, across, first)
     hop5.wait_recv()
     chip5 = passed(5, across, last)
-    for copy in copies_x:
-        copy.wait_recv()
-    copies_b = [send(rt.at[c, v], rt.at[c, v], b2_s.at[k], b2_r.at[k], peers_z[k]) for k in range(NZ - 1)]
-    pending += copies_b
+    received(leaf_x)
+    leaf_u = same(leaves.at[c, :, :, spot, :], b2_s, b2_r, peers_y)
     chip4.wait_recv()
     chip5.wait_recv()
     cross_gram(3)
     cross_gram(4)
-    sums.append(first_sum(1))
+    far = scatter(1)
+    near = spread(0, near)
+    far = spread(1, far)
+    near = along_x(0, near)
+    received(leaf_u)
+    over = send(leaves.at[c], leaves.at[c], b4_s, b4_r, partner)
+    pending.append(over)
+    near = along_u(0, near)
+    far = along_x(1, far)
+    over.wait_recv()
+
+    def leaf(o):
+        gx, gc = at(o)
+        return jnp.concatenate([leaves[gc, 0, gx], leaves[gc, 1, gx]], 0)
+
+    def at(o):
+        g = (tm - o + 8) % 8
+        return g // NC, g % NC
+
+    for o in (0, 4):
+        some, images = inverse_roots([leaf(o + i) for i in range(4)])
+        for i in range(4):
+            roots[o + i] = some[i]
+            roots[8 + o + i] = images[i]
+        if o == 0:
+            far = along_u(1, far)
     hop3.wait_recv()
     chip3 = passed(3, right, first)
-    pending += sums[0] + sums[1]
-    total = part[:, :, rows_of(u, 8), :]
-    for k in range(NY - 1):
-        sums[0][k].wait_recv()
-        sums[1][k].wait_recv()
-        total += rsy[k]
-    zsrc[...] = total.reshape(NZ, 8, N)
-    copies = [
-        send(zsrc.at[(v + k) % NZ], rsz.at[k - 1], z_s.at[k - 1], z_r.at[k - 1], peers_z[k - 1]) for k in range(1, NZ)
-    ]
-    total = zsrc[v]
-    for k, copy in enumerate(copies):
-        copy.wait_recv()
-        total += rsz[k]
-    pending += copies
-    spot = rows_of(u, 8)
-    kall[c, v, x, spot, :] = total
-    copies = [
-        send(kall.at[c, v, x, spot, :], kall.at[c, v, x, spot, :], p1_s.at[k], p1_r.at[k], peers_x[k])
-        for k in range(NX - 1)
-    ]
-    for copy in copies:
-        copy.wait_recv()
-    pending += copies
-    copies = [
-        send(kall.at[c, v, :, spot, :], kall.at[c, v, :, spot, :], p2_s.at[k], p2_r.at[k], peers_z[k])
-        for k in range(NZ - 1)
-    ]
-    for copy in copies:
-        copy.wait_recv()
-    pending += copies
-    by_d = []
-    for d in range(4):
-        pair = pl.ds(2 * d, 2)
-        by_d.append(
-            [
-                send(kall.at[c, pair, :, spot, :], kall.at[c, pair, :, spot, :], p3_s.at[d, k], p3_r.at[d, k], peers_y[k])
-                for k in range(NY - 1)
-            ]
-        )
-    for copy in copies_b:
-        copy.wait_recv()
-    swap = send(rt.at[c], rt.at[c], b4_s, b4_r, partner)
-    pending.append(swap)
+    overs = [swap(0, near[0]), swap(1, near[1])]
 
     def gate(d):
-        pair = pl.ds(2 * d, 2)
-        for copy in by_d[d]:
-            copy.wait_recv()
-        over = send(kall.at[c, pair], kall.at[c, pair], p4_s.at[d], p4_r.at[d], partner)
-        if d == 0:
-            swap.wait_recv()
+        if d == 2:
+            overs.extend([swap(2, far[0]), swap(3, far[1])])
         if d == 3:
             chip1.wait_recv()
             chip3.wait_recv()
-        over.wait_recv()
-        pending.append(over)
-        pending.extend(by_d[d])
-
-    def at(o):
-        g = (tm - o + 8) % 8
-        return g // NC, g % NC
-
-    def leaf(which, o):
-        gx, gc = at(o)
-        return rt[gc, :, gx, which].reshape(N, N)
+        overs[d].wait_recv()
 
     def stored(o, d):
         gx, gc = at(o)
@@ -349,10 +342,10 @@
         return xall[gx, gc]
 
     coef_ref[...], def_ref[...] = tree(
-        functools.partial(leaf, 0),
-        functools.partial(leaf, 1),
+        lambda o: roots[o],
+        lambda o: roots[8 + o],
         block,
-        own[...].reshape(N, N),
+        leaf(0),
         lambda level: sk_ref[level],
         x_of,
         gate,
@@ -364,21 +357,19 @@
 def body(snapshots, sketches):
     dma = pltpu.SemaphoreType.DMA
     vmem = pl.BlockSpec(memory_space=pltpu.VMEM)
-    counts = [6, 6, 7, 7, (2, 7), (2, 7), 7, 7, 3, 3, 7, 7, (4, 7), (4, 7), 4, 4, 7, 7, 7, 7, 7, 7, 3, 3, 7, 7]
+    counts = [6, 6, 7, 7, (2, 7), (2, 7), (2, 7), (2, 7), (2, 3), (2, 3), (4, 7), (4, 7), 4, 4, 7, 7, 7, 7, 3, 3, 7, 7]
     shapes = [
         (ROWS, N),
         (NX, NC, ROWS, N),
         (NC, NZ, NX, 64, N),
-        (NC, NZ, NX, 2, 16, N),
-        (2, 64, N),
+        (NC, 2, NX, 64, N),
+        (16, N, N),
         (4, 2, 64, N),
-        (NY - 1, 4, 2, 8, N),
-        (NZ - 1, 8, N),
-        (NZ, 8, N),
+        (2, NY - 1, 2, 2, 8, N),
+        (2, NZ, 4, 8, N),
         (2, 64, N),
         (NY - 1, 2, 8, N),
         (NZ, 2, 8, N),
-        (2, N, N),
     ]
     turned, removed = pl.pallas_call(
         step,

time: 99.9 us -> 87.1 us (0.87)
  Pallas kernels: 95.6 us -> 82.8 us
    pallas_call x1, Pallas kernels: 95.6 us -> 82.8 us  [body(): pl.pallas_call(step, out_shape=[jax.ShapeDtypeStruct((N, N), F32), jax.Sh...]
where the time goes in v4:
time: 87.1 us; the launch traced here: 86.9 us
  Pallas kernels  82.8 us (95%)
  other arithmetic  1.89 us (2%)
  local copies, waits for them, and re-layouts  1.57 us (2%)
    pallas_call x1, Pallas kernels, body(): pl.pallas_call(step, out_shape=[jax.ShapeDtypeStruct((N, N), F32), jax.Sh...  82.8 us
    sub x1, other arithmetic, body(): return (turned.T, snapshots - removed)  1.89 us

profile of v4, /device:TPU:1, one launch (start us, length us, event | category | flops | bytes accessed | tf_op | source)
XLA Modules:
  0.0 86.9 jit_solution(3428513978623748600)
XLA Ops:
  0.6 0.0 copy-start
  0.6 82.8 %step.1 = (f32[128,128]{1,0:T(8,128)}, f32[1024,128]{1,0:T(8,128)}) custom-call(f32[1024,128]{1,0:T(8,128)} %x_hbm.1, f32[3,256,128]{2,1,0:T(8,128)} %sk_ref.1), custom_call_target="tpu_custom_call" | custom-call | tf_op jit(solution)/shard_map/step/pallas_call | solution.py:374
  83.4 1.6 %copy.4 = f32[128,128]{1,0:T(8,128)} copy(f32[128,128]{0,1:T(8,128)} %bitcast.1) | data formatting | bytes 131072
  85.0 0.0 copy-done
  85.0 1.9 %sub.3 = f32[1024,128]{1,0:T(8,128)} subtract(f32[1024,128]{1,0:T(8,128)S(1)} %copy-done, f32[1024,128]{1,0:T(8,128)} %get-tuple-element.5) | non-fusion elementwise | flops 131072 | bytes 1572864 | tf_op jit(solution)/shard_map/sub | solution.py:389
Async XLA Ops:
  0.6 84.3 %copy-start = (f32[1024,128]{1,0:T(8,128)S(1)}, f32[1024,128]{1,0:T(8,128)}, u32[]{:S(2)}) copy-start(f32[1024,128]{1,0:T(8,128)} %x_hbm.1) | copy-start | bytes 1572868

commit v5 on v4

--- a/solution.py
+++ b/solution.py
@@ -43,9 +43,9 @@
         if step == 4 and not want_image:
             zs = [mm(z, m) for z, m in zip(zs, ms)]
         else:
-            both = [mm(jnp.concatenate([t, z], 0), m) for t, z, m in zip(ts, zs, ms)]
-            zs = [b[N:] for b in both]
-            ts = [mm(b[:N], m) for b, m in zip(both, ms)]
+            both = [mm(m, jnp.concatenate([t, z], 1)) for t, z, m in zip(ts, zs, ms)]
+            zs = [b[:, N:] for b in both]
+            ts = [mm(b[:, :N], m) for b, m in zip(both, ms)]
     return [z / jnp.sqrt(s) for z, s in zip(zs, scales)], ts
 
 
@@ -57,7 +57,7 @@
     return s, mm(s.T, mm(gram, s))
 
 
-def tree(root, image, block, own, sketch, x_of, gate):
+def tree(root, image, block, own, sketch, halves, gate):
     gate(0)
     r = [root(o) for o in range(8)]
     s0, a0, e0 = [], [], []
@@ -97,8 +97,10 @@
     h = mm(jnp.concatenate([mm(w_far, r2[1]), mm(w_near, r2[0])], 1), s2)
     upper = mm(e1[1], mm(r2[1], s2[:N]))
     lower = mm(e1[0], mm(r2[0], s2[N:]))
-    x_all = jnp.concatenate([x_of(o) for o in range(7, -1, -1)], 1)
-    base = mm(x_all, jnp.concatenate([upper, lower], 0))
+    high, low = halves()
+    mix_h, mix_l = split(jnp.concatenate([upper, lower], 0))
+    wide = jnp.concatenate([high, high, low], 1)
+    base = jnp.dot(wide, jnp.concatenate([mix_h, mix_l, mix_h], 0), preferred_element_type=F32)
     r3 = inverse_roots([a2], False)[0][0]
     turned = mm(h, r3)
     return turned, mm(base, mm(r3, turned.T))
@@ -120,7 +122,7 @@
     return pl.ds(pl.multiple_of(index * count, count), count)
 
 
-def step(x_hbm, sk_ref, coef_ref, def_ref, x_ref, xall, kall, leaves, roots, part, rsy, rsz, lrow, lsy, lsz,
+def step(x_hbm, sk_ref, coef_ref, def_ref, x_ref, xall, xh, xl, kall, leaves, roots, part, rsy, rsz, lrow, lsy, lsz,
          g_s, g_r, c_s, c_r, y_s, y_r, z_s, z_r, p1_s, p1_r, p3_s, p3_r, p4_s, p4_r,
          ly_s, ly_r, lz_s, lz_r, b1_s, b1_r, b2_s, b2_r, b4_s, b4_r, load_s):
     x, c, u, v = place()
@@ -142,6 +144,8 @@
     mine = x_ref[...]
     xall[x, c] = mine
     mine_h, mine_l = split(mine)
+    xh[0] = mine_h
+    xl[0] = mine_l
     turned_h, turned_l = split(mine.T)
     turned = jnp.concatenate([turned_h, turned_h, turned_l], 1)
 
@@ -211,6 +215,10 @@
 
     spot = rows_of(u, 8)
 
+    def at(o):
+        g = (tm - o + 8) % 8
+        return g // NC, g % NC
+
     def to_line(src, dst, s, r, peers):
         return [send(src, dst, s.at[k], r.at[k], peer) for k, peer in enumerate(peers)]
 
@@ -227,10 +235,15 @@
     hop2.wait_recv()
     chip2 = passed(2, left, last)
 
+    def prepare(o):
+        gx, gc = at(o)
+        high, low = split(xall[gx, gc])
+        xh[o] = high
+        xl[o] = low
+        return high, low
+
     def cross_gram(d):
-        other = (2 * x + c - d + 8) % 8
-        high, low = split(xall[other // NC, other % NC])
-        part[d - 1] = gram_with(high, low).reshape(2, 64, N)
+        part[d - 1] = gram_with(*prepare(d)).reshape(2, 64, N)
 
     def scatter(half):
         pair = pl.ds(2 * half, 2)
@@ -286,6 +299,7 @@
     chip4 = passed(4, across, first)
     hop5.wait_recv()
     chip5 = passed(5, across, last)
+    near = spread(0, near)
     received(leaf_x)
     leaf_u = same(leaves.at[c, :, :, spot, :], b2_s, b2_r, peers_y)
     chip4.wait_recv()
@@ -293,41 +307,43 @@
     cross_gram(3)
     cross_gram(4)
     far = scatter(1)
-    near = spread(0, near)
+    hop3.wait_recv()
+    chip3 = passed(3, right, first)
+    near = along_x(0, near)
     far = spread(1, far)
-    near = along_x(0, near)
     received(leaf_u)
     over = send(leaves.at[c], leaves.at[c], b4_s, b4_r, partner)
     pending.append(over)
     near = along_u(0, near)
-    far = along_x(1, far)
     over.wait_recv()
 
     def leaf(o):
         gx, gc = at(o)
         return jnp.concatenate([leaves[gc, 0, gx], leaves[gc, 1, gx]], 0)
 
-    def at(o):
-        g = (tm - o + 8) % 8
-        return g // NC, g % NC
-
-    for o in (0, 4):
-        some, images = inverse_roots([leaf(o + i) for i in range(4)])
+    def leaf_roots(first_o):
+        some, images = inverse_roots([leaf(first_o + i) for i in range(4)])
         for i in range(4):
-            roots[o + i] = some[i]
-            roots[8 + o + i] = images[i]
-        if o == 0:
-            far = along_u(1, far)
-    hop3.wait_recv()
-    chip3 = passed(3, right, first)
-    overs = [swap(0, near[0]), swap(1, near[1])]
+            roots[first_o + i] = some[i]
+            roots[8 + first_o + i] = images[i]
+
+    leaf_roots(0)
+    far = along_x(1, far)
+    leaf_roots(4)
+    overs = [swap(0, near[0])]
+    far = along_u(1, far)
+    chip1.wait_recv()
+    chip3.wait_recv()
+    for o in (5, 6, 7):
+        prepare(o)
 
     def gate(d):
+        if d == 1:
+            overs.append(swap(1, near[1]))
         if d == 2:
-            overs.extend([swap(2, far[0]), swap(3, far[1])])
+            overs.append(swap(2, far[0]))
         if d == 3:
-            chip1.wait_recv()
-            chip3.wait_recv()
+            overs.append(swap(3, far[1]))
         overs[d].wait_recv()
 
     def stored(o, d):
@@ -337,9 +353,8 @@
     def block(a, b):
         return stored(a, b - a) if b - a <= 4 else stored(b, 8 - b + a).T
 
-    def x_of(o):
-        gx, gc = at(o)
-        return xall[gx, gc]
+    def halves():
+        return [jnp.concatenate([ref[o] for o in range(7, -1, -1)], 1) for ref in (xh, xl)]
 
     coef_ref[...], def_ref[...] = tree(
         lambda o: roots[o],
@@ -347,11 +362,16 @@
         block,
         leaf(0),
         lambda level: sk_ref[level],
-        x_of,
+        halves,
         gate,
     )
     for copy in pending:
         copy.wait_send()
+
+
+def outputs(x_ref, removed_ref, turned_ref, coefficients_ref, deflated_ref):
+    coefficients_ref[...] = turned_ref[...].T
+    deflated_ref[...] = x_ref[...] - removed_ref[...]
 
 
 def body(snapshots, sketches):
@@ -359,8 +379,6 @@
     vmem = pl.BlockSpec(memory_space=pltpu.VMEM)
     counts = [6, 6, 7, 7, (2, 7), (2, 7), (2, 7), (2, 7), (2, 3), (2, 3), (4, 7), (4, 7), 4, 4, 7, 7, 7, 7, 3, 3, 7, 7]
     shapes = [
-        (ROWS, N),
-        (NX, NC, ROWS, N),
         (NC, NZ, NX, 64, N),
         (NC, 2, NX, 64, N),
         (16, N, N),
@@ -377,6 +395,10 @@
         in_specs=[pl.BlockSpec(memory_space=pl.ANY), vmem],
         out_specs=[vmem] * 2,
         scratch_shapes=[
+            pltpu.VMEM((ROWS, N), F32),
+            pltpu.VMEM((NX, NC, ROWS, N), F32),
+            pltpu.VMEM((2 * NX, ROWS, N), BF),
+            pltpu.VMEM((2 * NX, ROWS, N), BF),
             *[pltpu.VMEM(s, F32) for s in shapes],
             *[dma(n if isinstance(n, tuple) else (n,)) for n in counts],
             dma,
@@ -386,7 +408,13 @@
         compiler_params=pltpu.CompilerParams(collective_id=0, has_side_effects=True, vmem_limit_bytes=60 << 20),
         name="step",
     )(snapshots, sketches)
-    return turned.T, snapshots - removed
+    return pl.pallas_call(
+        outputs,
+        out_shape=[jax.ShapeDtypeStruct((N, N), F32), jax.ShapeDtypeStruct((ROWS, N), F32)],
+        in_specs=[vmem] * 3,
+        out_specs=[vmem] * 2,
+        name="outputs",
+    )(snapshots, removed, turned)
 
 
 def solution(mesh):

time: 87.1 us -> 85.8 us (0.985)
  Pallas kernels: 82.8 us -> 84.9 us
  other arithmetic: 1.89 us -> 0 us
  local copies, waits for them, and re-layouts: 1.57 us -> 0 us
    pallas_call x0 -> x1, Pallas kernels: none -> 2.08 us  [body(): pl.pallas_call(outputs, out_shape=[jax.ShapeDtypeStruct((N, N), F32), jax...]
    sub x1 -> x0, other arithmetic: 1.89 us -> none  [body(): return (turned.T, snapshots - removed)]
    unnamed x3 -> x0, local copies, waits for them, and re-layouts: 1.57 us -> none
where the time goes in v5:
time: 85.8 us; the launch traced here: 85.6 us
  Pallas kernels  84.9 us (99%)
    pallas_call x1, Pallas kernels, body(): pl.pallas_call(step, out_shape=[jax.ShapeDtypeStruct((N, N), F32), jax.Sh...  82.8 us
    pallas_call x1, Pallas kernels, body(): pl.pallas_call(outputs, out_shape=[jax.ShapeDtypeStruct((N, N), F32), jax...  2.08 us

profile of v5, /device:TPU:1, one launch (start us, length us, event | category | flops | bytes accessed | tf_op | source)
XLA Modules:
  0.0 85.6 jit_solution(11282258454312617829)
XLA Ops:
  0.6 82.8 %step.1 = (f32[128,128]{1,0:T(8,128)}, f32[1024,128]{1,0:T(8,128)}) custom-call(f32[1024,128]{1,0:T(8,128)} %x_ref.1, f32[3,256,128]{2,1,0:T(8,128)} %sk_ref.1), custom_call_target="tpu_custom_call" | custom-call | tf_op jit(solution)/shard_map/step/pallas_call | solution.py:392
  83.5 2.1 %outputs.1 = (f32[128,128]{1,0:T(8,128)}, f32[1024,128]{1,0:T(8,128)}) custom-call(f32[1024,128]{1,0:T(8,128)} %x_ref.1, f32[1024,128]{1,0:T(8,128)} %get-tuple-element.4.removed_ref, f32[128,128]{1,0:T(8,128)} %get-tuple-element.5.turned_ref), custom_call_target="tpu_custom_call" | custom-call | tf_op jit(solution)/shard_map/outputs/pallas_call | solution.py:411

commit v6 on v5

--- a/solution.py
+++ b/solution.py
@@ -227,10 +227,9 @@
 
     received(copies)
     leaves[c, :, x, spot, :] = in_order(lsz)
-    leaf_x = same(leaves.at[c, :, x, spot, :], b1_s, b1_r, peers_x)
+    leaf_u = same(leaves.at[c, :, x, spot, :], b2_s, b2_r, peers_y)
     hop1.wait_recv()
     hop5 = hop(5, right, last, to_left)
-    hop3 = hop(3, x, first, to_left, x_ref.at[first])
     chip1 = passed(1, right, last)
     hop2.wait_recv()
     chip2 = passed(2, left, last)
@@ -269,11 +268,14 @@
             for k in range(NZ - 1)
         ]
 
-    def along_x(half, copies):
+    def own_rows(half, copies):
         received(copies)
         quad = pl.ds(4 * half, 4)
         kall[c, quad, x, spot, :] = in_order(rsz.at[half])
-        return same(kall.at[c, quad, x, spot, :], p1_s.at[half], p1_r.at[half], peers_x)
+        return kall.at[c, quad, x, spot, :]
+
+    def along_x(half, copies):
+        return same(own_rows(half, copies), p1_s.at[0], p1_r.at[0], peers_x)
 
     def along_u(half, copies):
         received(copies)
@@ -282,6 +284,13 @@
             for d in (2 * half, 2 * half + 1)
         ]
 
+    def own_along_u(copies):
+        return same(own_rows(1, copies), p3_s.at[2], p3_r.at[2], peers_y)
+
+    def whole_along_x(copies):
+        received(copies)
+        return [same(kall.at[c, pl.ds(2 * d, 2), x], p1_s.at[d - 1], p1_r.at[d - 1], peers_x) for d in (2, 3)]
+
     def swap(d, copies):
         received(copies)
         pair = pl.ds(2 * d, 2)
@@ -295,26 +304,24 @@
     cross_gram(1)
     cross_gram(2)
     near = scatter(0)
+    received(leaf_u)
+    leaf_x = same(leaves.at[c, :, x], b1_s, b1_r, peers_x)
+    hop3 = hop(3, x, first, to_left, x_ref.at[first])
     hop4.wait_recv()
     chip4 = passed(4, across, first)
     hop5.wait_recv()
     chip5 = passed(5, across, last)
     near = spread(0, near)
-    received(leaf_x)
-    leaf_u = same(leaves.at[c, :, :, spot, :], b2_s, b2_r, peers_y)
     chip4.wait_recv()
     chip5.wait_recv()
     cross_gram(3)
     cross_gram(4)
     far = scatter(1)
-    hop3.wait_recv()
-    chip3 = passed(3, right, first)
+    received(leaf_x)
+    over = send(leaves.at[c], leaves.at[c], b4_s, b4_r, partner)
+    pending.append(over)
     near = along_x(0, near)
     far = spread(1, far)
-    received(leaf_u)
-    over = send(leaves.at[c], leaves.at[c], b4_s, b4_r, partner)
-    pending.append(over)
-    near = along_u(0, near)
     over.wait_recv()
 
     def leaf(o):
@@ -328,14 +335,17 @@
             roots[8 + first_o + i] = images[i]
 
     leaf_roots(0)
-    far = along_x(1, far)
+    near = along_u(0, near)
     leaf_roots(4)
-    overs = [swap(0, near[0])]
-    far = along_u(1, far)
+    far = own_along_u(far)
+    hop3.wait_recv()
+    chip3 = passed(3, right, first)
     chip1.wait_recv()
     chip3.wait_recv()
     for o in (5, 6, 7):
         prepare(o)
+    overs = [swap(0, near[0])]
+    far = whole_along_x(far)
 
     def gate(d):
         if d == 1:
@@ -377,7 +387,7 @@
 def body(snapshots, sketches):
     dma = pltpu.SemaphoreType.DMA
     vmem = pl.BlockSpec(memory_space=pltpu.VMEM)
-    counts = [6, 6, 7, 7, (2, 7), (2, 7), (2, 7), (2, 7), (2, 3), (2, 3), (4, 7), (4, 7), 4, 4, 7, 7, 7, 7, 3, 3, 7, 7]
+    counts = [6, 6, 7, 7, (2, 7), (2, 7), (2, 7), (2, 7), (3, 3), (3, 3), (3, 7), (3, 7), 4, 4, 7, 7, 7, 7, 3, 3, 7, 7]
     shapes = [
         (NC, NZ, NX, 64, N),
         (NC, 2, NX, 64, N),

time: 85.8 us -> 86 us (level)
  no operation moved by 1% of the time
where the time goes in v6:
time: 86 us; the launch traced here: 85.8 us
  Pallas kernels  85.1 us (99%)
    pallas_call x1, Pallas kernels, body(): pl.pallas_call(step, out_shape=[jax.ShapeDtypeStruct((N, N), F32), jax.Sh...  83 us
    pallas_call x1, Pallas kernels, body(): pl.pallas_call(outputs, out_shape=[jax.ShapeDtypeStruct((N, N), F32), jax...  2.08 us

profile of v6, /device:TPU:1, one launch (start us, length us, event | category | flops | bytes accessed | tf_op | source)
XLA Modules:
  0.0 85.8 jit_solution(12046338819493946272)
XLA Ops:
  0.6 83.0 %step.1 = (f32[128,128]{1,0:T(8,128)}, f32[1024,128]{1,0:T(8,128)}) custom-call(f32[1024,128]{1,0:T(8,128)} %x_ref.1, f32[3,256,128]{2,1,0:T(8,128)} %sk_ref.1), custom_call_target="tpu_custom_call" | custom-call | tf_op jit(solution)/shard_map/step/pallas_call | solution.py:402
  83.7 2.1 %outputs.1 = (f32[128,128]{1,0:T(8,128)}, f32[1024,128]{1,0:T(8,128)}) custom-call(f32[1024,128]{1,0:T(8,128)} %x_ref.1, f32[1024,128]{1,0:T(8,128)} %get-tuple-element.4.removed_ref, f32[128,128]{1,0:T(8,128)} %get-tuple-element.5.turned_ref), custom_call_target="tpu_custom_call" | custom-call | tf_op jit(solution)/shard_map/outputs/pallas_call | solution.py:421

commit v7 on v6

--- a/solution.py
+++ b/solution.py
@@ -68,8 +68,8 @@
         a0.append(a)
     for j in range(4):
         e0.append(jnp.concatenate([mm(r[2 * j + 1], s0[j][:N]), mm(r[2 * j], s0[j][N:])], 0))
+    gate(1)
     r1, t1 = inverse_roots(a0)
-    gate(1)
     gate(2)
     cross1 = []
     for j in range(0, 4, 2):
@@ -348,13 +348,13 @@
     far = whole_along_x(far)
 
     def gate(d):
-        if d == 1:
-            overs.append(swap(1, near[1]))
         if d == 2:
-            overs.append(swap(2, far[0]))
-        if d == 3:
             overs.append(swap(3, far[1]))
         overs[d].wait_recv()
+        if d == 0:
+            overs.append(swap(1, near[1]))
+        if d == 1:
+            overs.append(swap(2, far[0]))
 
     def stored(o, d):
         gx, gc = at(o)

time: 86 us -> 85.4 us (level)
  no operation moved by 1% of the time
where the time goes in v7:
time: 85.4 us; the launch traced here: 85.2 us
  Pallas kernels  84.5 us (99%)
    pallas_call x1, Pallas kernels, body(): pl.pallas_call(step, out_shape=[jax.ShapeDtypeStruct((N, N), F32), jax.Sh...  82.5 us
    pallas_call x1, Pallas kernels, body(): pl.pallas_call(outputs, out_shape=[jax.ShapeDtypeStruct((N, N), F32), jax...  2.08 us

profile of v7, /device:TPU:1, one launch (start us, length us, event | category | flops | bytes accessed | tf_op | source)
XLA Modules:
  0.0 85.2 jit_solution(17629132567065124737)
XLA Ops:
  0.6 82.5 %step.1 = (f32[128,128]{1,0:T(8,128)}, f32[1024,128]{1,0:T(8,128)}) custom-call(f32[1024,128]{1,0:T(8,128)} %x_ref.1, f32[3,256,128]{2,1,0:T(8,128)} %sk_ref.1), custom_call_target="tpu_custom_call" | custom-call | tf_op jit(solution)/shard_map/step/pallas_call | solution.py:402
  83.1 2.1 %outputs.1 = (f32[128,128]{1,0:T(8,128)}, f32[1024,128]{1,0:T(8,128)}) custom-call(f32[1024,128]{1,0:T(8,128)} %x_ref.1, f32[1024,128]{1,0:T(8,128)} %get-tuple-element.4.removed_ref, f32[128,128]{1,0:T(8,128)} %get-tuple-element.5.turned_ref), custom_call_target="tpu_custom_call" | custom-call | tf_op jit(solution)/shard_map/outputs/pallas_call | solution.py:421

commit v8 on v7

--- a/solution.py
+++ b/solution.py
@@ -32,13 +32,15 @@
     return jnp.where(down == across, 1.0, 0.0).astype(F32)
 
 
-def inverse_roots(grams, want_image=True):
+def inverse_roots(grams, want_image=True, midway=None):
     one = identity()
     scales = [jnp.sqrt(jnp.sum(a * a, keepdims=True) + 1e-06) for a in grams]
     ts = [a / s for a, s in zip(grams, scales)]
     zs = ms = [1.5 * one - 0.5 * t for t in ts]
     ts = [mm(mm(t, m), m) for t, m in zip(ts, ms)]
     for step in range(1, 5):
+        if step == 3 and midway is not None:
+            midway()
         ms = [1.5 * one - 0.5 * t for t in ts]
         if step == 4 and not want_image:
             zs = [mm(z, m) for z, m in zip(zs, ms)]
@@ -53,8 +55,9 @@
     top = jnp.concatenate([t_p, cross.T], 1)
     bottom = jnp.concatenate([cross, t_g], 1)
     gram = jnp.concatenate([top, bottom], 0)
-    s = mm(gram, sketch)
-    return s, mm(s.T, mm(gram, s))
+    s_t = mm(sketch.T, gram)
+    s = s_t.T
+    return s, mm(mm(s_t, gram), s)
 
 
 def tree(root, image, block, own, sketch, halves, gate):
@@ -68,8 +71,7 @@
         a0.append(a)
     for j in range(4):
         e0.append(jnp.concatenate([mm(r[2 * j + 1], s0[j][:N]), mm(r[2 * j], s0[j][N:])], 0))
-    gate(1)
-    r1, t1 = inverse_roots(a0)
+    r1, t1 = inverse_roots(a0, midway=lambda: gate(1))
     gate(2)
     cross1 = []
     for j in range(0, 4, 2):
@@ -284,12 +286,16 @@
             for d in (2 * half, 2 * half + 1)
         ]
 
-    def own_along_u(copies):
-        return same(own_rows(1, copies), p3_s.at[2], p3_r.at[2], peers_y)
-
-    def whole_along_x(copies):
-        received(copies)
-        return [same(kall.at[c, pl.ds(2 * d, 2), x], p1_s.at[d - 1], p1_r.at[d - 1], peers_x) for d in (2, 3)]
+    def far_first(copies):
+        own_rows(1, copies)
+        by_x = same(kall.at[c, pl.ds(4, 2), x, spot, :], p1_s.at[1], p1_r.at[1], peers_x)
+        return by_x, same(kall.at[c, pl.ds(6, 2), x, spot, :], p3_s.at[3], p3_r.at[3], peers_y)
+
+    def far_last(by_x, by_u):
+        received(by_x)
+        by_x = same(kall.at[c, pl.ds(4, 2), :, spot, :], p3_s.at[2], p3_r.at[2], peers_y)
+        received(by_u)
+        return by_x, same(kall.at[c, pl.ds(6, 2), x], p1_s.at[2], p1_r.at[2], peers_x)
 
     def swap(d, copies):
         received(copies)
@@ -337,15 +343,15 @@
     leaf_roots(0)
     near = along_u(0, near)
     leaf_roots(4)
-    far = own_along_u(far)
+    far = far_first(far)
     hop3.wait_recv()
     chip3 = passed(3, right, first)
     chip1.wait_recv()
+    far = far_last(*far)
     chip3.wait_recv()
     for o in (5, 6, 7):
         prepare(o)
     overs = [swap(0, near[0])]
-    far = whole_along_x(far)
 
     def gate(d):
         if d == 2:
@@ -387,7 +393,7 @@
 def body(snapshots, sketches):
     dma = pltpu.SemaphoreType.DMA
     vmem = pl.BlockSpec(memory_space=pltpu.VMEM)
-    counts = [6, 6, 7, 7, (2, 7), (2, 7), (2, 7), (2, 7), (3, 3), (3, 3), (3, 7), (3, 7), 4, 4, 7, 7, 7, 7, 3, 3, 7, 7]
+    counts = [6, 6, 7, 7, (2, 7), (2, 7), (2, 7), (2, 7), (3, 3), (3, 3), (4, 7), (4, 7), 4, 4, 7, 7, 7, 7, 3, 3, 7, 7]
     shapes = [
         (NC, NZ, NX, 64, N),
         (NC, 2, NX, 64, N),

time: 85.4 us -> 82.8 us (0.970)
  Pallas kernels: 84.5 us -> 81.9 us
    pallas_call x1, Pallas kernels: 82.5 us -> 79.8 us  [body(): pl.pallas_call(step, out_shape=[jax.ShapeDtypeStruct((N, N), F32), jax.Sh...]
where the time goes in v8:
time: 82.8 us; the launch traced here: 82.5 us
  Pallas kernels  81.9 us (99%)
    pallas_call x1, Pallas kernels, body(): pl.pallas_call(step, out_shape=[jax.ShapeDtypeStruct((N, N), F32), jax.Sh...  79.8 us
    pallas_call x1, Pallas kernels, body(): pl.pallas_call(outputs, out_shape=[jax.ShapeDtypeStruct((N, N), F32), jax...  2.08 us

profile of v8, /device:TPU:1, one launch (start us, length us, event | category | flops | bytes accessed | tf_op | source)
XLA Modules:
  0.0 82.5 jit_solution(14027593294409871166)
XLA Ops:
  0.6 79.8 %step.1 = (f32[128,128]{1,0:T(8,128)}, f32[1024,128]{1,0:T(8,128)}) custom-call(f32[1024,128]{1,0:T(8,128)} %x_ref.1, f32[3,256,128]{2,1,0:T(8,128)} %sk_ref.1), custom_call_target="tpu_custom_call" | custom-call | tf_op jit(solution)/shard_map/step/pallas_call | solution.py:408
  80.5 2.1 %outputs.1 = (f32[128,128]{1,0:T(8,128)}, f32[1024,128]{1,0:T(8,128)}) custom-call(f32[1024,128]{1,0:T(8,128)} %x_ref.1, f32[1024,128]{1,0:T(8,128)} %get-tuple-element.4.removed_ref, f32[128,128]{1,0:T(8,128)} %get-tuple-element.5.turned_ref), custom_call_target="tpu_custom_call" | custom-call | tf_op jit(solution)/shard_map/outputs/pallas_call | solution.py:427

commit v9 on v8

--- a/solution.py
+++ b/solution.py
@@ -291,11 +291,13 @@
         by_x = same(kall.at[c, pl.ds(4, 2), x, spot, :], p1_s.at[1], p1_r.at[1], peers_x)
         return by_x, same(kall.at[c, pl.ds(6, 2), x, spot, :], p3_s.at[3], p3_r.at[3], peers_y)
 
-    def far_last(by_x, by_u):
-        received(by_x)
-        by_x = same(kall.at[c, pl.ds(4, 2), :, spot, :], p3_s.at[2], p3_r.at[2], peers_y)
-        received(by_u)
-        return by_x, same(kall.at[c, pl.ds(6, 2), x], p1_s.at[2], p1_r.at[2], peers_x)
+    def third_along_u(copies):
+        received(copies)
+        return same(kall.at[c, pl.ds(4, 2), :, spot, :], p3_s.at[2], p3_r.at[2], peers_y)
+
+    def fourth_along_x(copies):
+        received(copies)
+        return same(kall.at[c, pl.ds(6, 2), x], p1_s.at[2], p1_r.at[2], peers_x)
 
     def swap(d, copies):
         received(copies)
@@ -343,24 +345,25 @@
     leaf_roots(0)
     near = along_u(0, near)
     leaf_roots(4)
-    far = far_first(far)
+    third, fourth = far_first(far)
     hop3.wait_recv()
     chip3 = passed(3, right, first)
     chip1.wait_recv()
-    far = far_last(*far)
     chip3.wait_recv()
     for o in (5, 6, 7):
         prepare(o)
+    third = third_along_u(third)
     overs = [swap(0, near[0])]
+    fourth = fourth_along_x(fourth)
 
     def gate(d):
         if d == 2:
-            overs.append(swap(3, far[1]))
+            overs.append(swap(3, fourth))
         overs[d].wait_recv()
         if d == 0:
             overs.append(swap(1, near[1]))
         if d == 1:
-            overs.append(swap(2, far[0]))
+            overs.append(swap(2, third))
 
     def stored(o, d):
         gx, gc = at(o)

time: 82.8 us -> 82.1 us (level)
  no operation moved by 1% of the time
where the time goes in v9:
time: 82.1 us; the launch traced here: 81.8 us
  Pallas kernels  81.2 us (99%)
    pallas_call x1, Pallas kernels, body(): pl.pallas_call(step, out_shape=[jax.ShapeDtypeStruct((N, N), F32), jax.Sh...  79.1 us
    pallas_call x1, Pallas kernels, body(): pl.pallas_call(outputs, out_shape=[jax.ShapeDtypeStruct((N, N), F32), jax...  2.08 us

profile of v9, /device:TPU:1, one launch (start us, length us, event | category | flops | bytes accessed | tf_op | source)
XLA Modules:
  0.0 81.8 jit_solution(15850173846318525161)
XLA Ops:
  0.6 79.1 %step.1 = (f32[128,128]{1,0:T(8,128)}, f32[1024,128]{1,0:T(8,128)}) custom-call(f32[1024,128]{1,0:T(8,128)} %x_ref.1, f32[3,256,128]{2,1,0:T(8,128)} %sk_ref.1), custom_call_target="tpu_custom_call" | custom-call | tf_op jit(solution)/shard_map/step/pallas_call | solution.py:411
  79.7 2.1 %outputs.1 = (f32[128,128]{1,0:T(8,128)}, f32[1024,128]{1,0:T(8,128)}) custom-call(f32[1024,128]{1,0:T(8,128)} %x_ref.1, f32[1024,128]{1,0:T(8,128)} %get-tuple-element.4.removed_ref, f32[128,128]{1,0:T(8,128)} %get-tuple-element.5.turned_ref), custom_call_target="tpu_custom_call" | custom-call | tf_op jit(solution)/shard_map/outputs/pallas_call | solution.py:430
